TPU v7x, 256 devices: a whole 4x4x8 slice. The times are simulated.
256 devices in a mesh: noise: 8 (over z), dp: 32 (over x, y, core).
Axes of the slice: x: 4, y: 4, z: 8, core: 2. Of those that a mesh axis runs over, the one named last changes fastest.
Arguments:
- noise_points: float32 [12288, 512], P('noise'), may hold values from -1.5 to 1.5
- data_points: float32 [12288, 512], P('dp', 'noise'), may hold values from -1.5 to 1.5
- noise_blocks: int32 [8], P('noise'), may hold values from 1 to 12, as said below
- data_blocks: int32 [32], P('dp'), may hold values from 1 to 3, as said below
Outputs:
- noise_potential: float32 [12288], P('noise')
- data_potential: float32 [12288], P('dp')
- noise_target: float32 [512, 12288], P('dp', 'noise')
- data_target: float32 [512, 12288], P('noise', 'dp')
Inputs may be any that keep to these rules, and one draw needn't show every extreme that they name: `noise_blocks`: blocks 0 up to this count of each device's 12 slots are live, the rest padding; some device has all 12 live. `data_blocks`: blocks 0 up to this count of each device's 3 slots are live, the rest padding; some device has all 3 live.
All inputs are finite; a program needn't handle non-finite values.
Results may differ from a plain program's by a relative error of at most 0.0003.
Values sent between devices are 32-bit elements; how exact they have to be, the bound alone decides.
No kernel may reach another device: no remote copies, remote signals or barrier semaphores. Data moves between devices by JAX's collectives and lax.ppermute only.
A program may use at most 64 MiB of HBM per device.

v0:
```python
import jax
import jax.numpy as jnp
from jax import lax
from jax.sharding import PartitionSpec as P

BLOCK = 128
ITERS = 3


SMOOTHING_TEMP = 0.125


def from_everyone(shard, axis):
    devices = lax.axis_size(axis)
    return lax.all_to_all(
        jnp.broadcast_to(shard[None], (devices, *shard.shape)), axis, 0, 0, tiled=True
    )


def gathered_once(shard, axis):
    leaves = jax.tree.leaves(shard)
    turns = sorted(range(len(leaves)), key=lambda k: -leaves[k].size)
    width = (1, *leaves[turns[0]].shape)[-1]
    lines = [
        jnp.pad(leaves[k].reshape(-1), (0, -leaves[k].size % width)).reshape(-1, width)
        for k in turns
    ]
    both, at, found = (from_everyone(jnp.concatenate(lines), axis), 0, {})
    for k, line in zip(turns, lines):
        piece = both[:, at : at + len(line)].reshape(len(both), -1)
        found[k] = piece[:, : leaves[k].size].reshape(-1, *leaves[k].shape)
        at += len(line)
    numbers = iter(range(len(leaves)))
    return jax.tree.map(lambda _: found[next(numbers)], shard)


def gathered_by_type(shard, axis):
    leaves, found = (jax.tree.leaves(shard), {})
    for initial, a in enumerate(leaves):
        if initial not in found:
            alike = [k for k, b in enumerate(leaves) if b.dtype == a.dtype]
            got = (
                gathered_once([leaves[k] for k in alike], axis)
                if len(alike) > 1
                else [from_everyone(a, axis)]
            )
            for k, b in zip(alike, got):
                found[k] = b
    numbers = iter(range(len(leaves)))
    return jax.tree.map(lambda _: found[next(numbers)], shard)


def combined_pairwise(pieces, combine):
    while len(jax.tree.leaves(pieces)[0]) > 1:
        pieces = jax.vmap(combine)(
            *(jax.tree.map(lambda part: part[side::2], pieces) for side in (0, 1))
        )
    return jax.tree.map(lambda part: part[0], pieces)


def joined_all(shard, axis, combine):
    pieces = gathered_by_type(shard, axis)
    return combined_pairwise(pieces, combine)


def of_everyone(shard, axis):
    everything = from_everyone(shard, axis)
    return jnp.sum(everything, axis=0)


def laid_out(parts, dim):
    parts = jnp.moveaxis(parts, 0, dim)
    dims = parts.shape
    return parts.reshape(*dims[:dim], dims[dim] * dims[dim + 1], *dims[dim + 2 :])


def gather_directly(shard, axis, dim):
    return laid_out(from_everyone(shard, axis), dim)


def in_blocks(shard, dim, devices):
    before, after = (shard.shape[:dim], shard.shape[dim + 1 :])
    return jnp.moveaxis(shard.reshape(*before, devices, -1, *after), dim, 0)


def sent_and_summed(shard, axis, dim):
    devices = lax.axis_size(axis)
    parts = lax.all_to_all(in_blocks(shard, dim, devices), axis, 0, 0, tiled=True)
    return jnp.sum(parts, axis=0)


def pair_cost(rows, cols, col_sq):
    row_sq = jnp.sum(rows * rows, axis=1)
    cross = jnp.dot(
        rows, cols.T, precision=lax.Precision.HIGHEST, preferred_element_type=jnp.float32
    )
    return row_sq[:, None] + col_sq[None, :] - 2.0 * cross


def combine_peaks(first, second):
    top = jnp.maximum(first[0], second[0])
    return (top, first[1] * jnp.exp(first[0] - top) + second[1] * jnp.exp(second[0] - top))


def row_threshold(pair_scores):
    local = jnp.max(pair_scores, axis=1)
    mass = jnp.sum(jnp.exp(pair_scores - local[:, None]), axis=1)
    top, mass = joined_all((local, mass), "dp", combine_peaks)
    return top + jnp.log(mass)


def column_level(pair_scores):
    local = jnp.max(pair_scores, axis=0)
    mass = jnp.sum(jnp.exp(pair_scores - local[None, :]), axis=0)
    top, mass = joined_all((local, mass), "noise", combine_peaks)
    return top + jnp.log(mass)


def on_device(noise_points, data_points, noise_blocks, data_blocks):
    rows_dev = noise_points.shape[0]
    cols_dev = data_points.shape[0]
    noise_total = of_everyone((noise_blocks * BLOCK).astype(jnp.float32), "noise")
    data_total = of_everyone((data_blocks * BLOCK).astype(jnp.float32), "dp")
    log_noise_mass = -jnp.log(noise_total[0])
    log_data_mass = -jnp.log(data_total[0])
    data_full = gather_directly(data_points, "noise", 1)
    row_active = jnp.arange(rows_dev, dtype=jnp.int32) < noise_blocks[0] * BLOCK
    column_active = jnp.arange(cols_dev, dtype=jnp.int32) < data_blocks[0] * BLOCK
    col_sq = jnp.sum(data_full * data_full, axis=1)
    transport_cost = pair_cost(noise_points, data_full, col_sq)
    data_potential = jnp.zeros((cols_dev,), jnp.float32)
    noise_potential = jnp.zeros((rows_dev,), jnp.float32)
    for turn in range(ITERS):
        pair_scores = jnp.where(
            column_active[None, :],
            (data_potential[None, :] - transport_cost) / SMOOTHING_TEMP + log_data_mass,
            -jnp.inf,
        )
        noise_potential = jnp.where(row_active, -SMOOTHING_TEMP * row_threshold(pair_scores), 0.0)
        pair_scores = jnp.where(
            row_active[:, None],
            (noise_potential[:, None] - transport_cost) / SMOOTHING_TEMP + log_noise_mass,
            -jnp.inf,
        )
        data_potential = jnp.where(column_active, -SMOOTHING_TEMP * column_level(pair_scores), 0.0)
    pair_scores = jnp.where(
        column_active[None, :],
        (data_potential[None, :] - transport_cost) / SMOOTHING_TEMP + log_data_mass,
        -jnp.inf,
    )
    level = row_threshold(pair_scores)
    both_live = row_active[:, None] & column_active[None, :]
    noise_weights = jnp.where(both_live, jnp.exp(pair_scores - level[:, None]), 0.0)
    data_weights = jnp.where(
        both_live,
        jnp.exp(
            (noise_potential[:, None] + data_potential[None, :] - transport_cost) / SMOOTHING_TEMP
            + log_noise_mass
        ),
        0.0,
    )
    coords = data_full
    noise_target = sent_and_summed(
        lax.dot_general(
            coords,
            noise_weights,
            (((0,), (1,)), ((), ())),
            precision=lax.Precision.HIGHEST,
            preferred_element_type=jnp.float32,
        ),
        "dp",
        0,
    )
    coords = noise_points
    data_target = sent_and_summed(
        lax.dot_general(
            coords,
            data_weights,
            (((0,), (0,)), ((), ())),
            precision=lax.Precision.HIGHEST,
            preferred_element_type=jnp.float32,
        ),
        "noise",
        0,
    )
    return (noise_potential, data_potential, noise_target, data_target)


def solution(mesh):
    return jax.shard_map(
        on_device,
        mesh=mesh,
        in_specs=(P("noise", None), P("dp", "noise"), P("noise"), P("dp")),
        out_specs=(P("noise"), P("dp"), P("dp", "noise"), P("noise", "dp")),
        check_vma=False,
    )
```

profile of v0, /device:TPU:1, one launch (start us, length us, event | category | flops | bytes accessed | tf_op | source)
XLA Modules:
  0.0 248.1 jit_solution(9474747758334028918)
XLA Ops:
  1.3 15.3 %all_to_all.62 = f32[32,1,1]{2,1,0:T(1,128)S(1)} all-to-all(f32[32,1,1]{2,1,0:T(1,128)S(1)} %broadcast_in_dim.87), channel_id=1, replica_groups=mesh['noise'=8,'dp'=32] {'dp'}, dimensions={0} | all-to-all | bytes 256 | tf_op jit(solution)/shard_map/all_to_all | solution.py:15
  16.6 1.8 broadcast_in_dim.84
  18.5 8.2 %all-to-all-start = ((f32[8,384,64]{1,2,0:T(8,128)}), f32[8,384,64]{1,2,0:T(8,128)S(1)}, u32[]{:S(2)}, u32[]{:S(2)}) async-start(f32[8,384,64]{1,2,0:T(8,128)} %broadcast_in_dim.84), calls=%async_computation | async-start | bytes 1572864 | tf_op jit(solution)/shard_map/all_to_all | solution.py:15
  27.3 2.2 multiply_reduce_fusion
  29.5 0.6 reduce_sum.119
  30.8 19.4 %all-to-all-done = f32[8,384,64]{1,2,0:T(8,128)S(1)} async-done(((f32[8,384,64]{1,2,0:T(8,128)}), f32[8,384,64]{1,2,0:T(8,128)S(1)}, u32[]{:S(2)}, u32[]{:S(2)}) %all-to-all-start) | async-done | bytes 786464 | tf_op jit(solution)/shard_map/all_to_all | solution.py:15
  50.2 0.6 broadcast_in_dim.159
  50.8 3.3 %all-to-all-start.3 = ((f32[8,1,1]{2,1,0:T(1,128)}), f32[8,1,1]{2,1,0:T(1,128)S(1)}, u32[]{:S(2)}, u32[]{:S(2)}) async-start(f32[8,1,1]{2,1,0:T(1,128)} %broadcast_in_dim.159), calls=%async_computation.3 | async-start | bytes 8192 | tf_op jit(solution)/shard_map/all_to_all | solution.py:15
  54.2 6.3 %fusion.10 = (f32[1536]{0:T(1024)S(1)}, f32[1536,384]{0,1:T(8,128)S(1)}) fusion(f32[]{:T(128)S(6)} %neg.6, pred[384]{0:T(512)(128)(4,1)S(1)} %iota_compare_fusion.1, f32[1536,512]{1,0:T(8,128)} %param.4, f32[384,512]{0,1:T(8,128)S(1)} %bitcast.61, f32[384]{0:T(512)S(1)} %fusion.33, f32[1536]{0:T(1024)S(1)} %multiply_reduce_fusion), kind=kOutput, calls=%fused_computation.28 | convolution fusion | flops 3628595712 | bytes 6305668 | tf_op jit(solution)/shard_map/dot_general | solution.py:94
  60.6 0.7 exponential_reduce_fusion.6
  61.3 0.8 broadcast_in_dim.156
  62.1 4.5 %all-to-all-start.2 = ((f32[32,2,1536]{2,1,0:T(2,128)}), f32[32,2,1536]{2,1,0:T(2,128)S(1)}, u32[]{:S(2)}, u32[]{:S(2)}) async-start(f32[32,2,1536]{2,1,0:T(2,128)} %broadcast_in_dim.156), calls=%async_computation.2 | async-start | bytes 786432 | tf_op jit(solution)/shard_map/all_to_all | solution.py:15
  66.6 0.6 reduce_sum.121
  67.9 9.1 %all-to-all-done.2 = f32[32,2,1536]{2,1,0:T(2,128)S(1)} async-done(((f32[32,2,1536]{2,1,0:T(2,128)}), f32[32,2,1536]{2,1,0:T(2,128)S(1)}, u32[]{:S(2)}, u32[]{:S(2)}) %all-to-all-start.2) | async-done | bytes 393248 | tf_op jit(solution)/shard_map/all_to_all | solution.py:15
  77.0 0.3 fusion.59
  77.3 0.7 slice.419
  78.0 0.7 slice.420
  78.7 1.0 multiply_add_fusion.3
  80.2 0.5 fusion.11
  80.7 0.7 exponential_reduce_fusion.5
  81.4 12.9 %all_to_all.63 = f32[8,2,384]{2,1,0:T(2,128)S(1)} all-to-all(f32[8,2,384]{2,1,0:T(2,128)S(1)} %broadcast_in_dim.160), channel_id=1, replica_groups=mesh['noise'=8,'dp'=32] {'noise'}, dimensions={0} | all-to-all | bytes 49152 | tf_op jit(solution)/shard_map/all_to_all | solution.py:15
  94.6 0.5 fusion.12
  95.1 0.7 exponential_reduce_fusion.4
  95.9 0.1 broadcast_in_dim.162
  96.0 15.0 %all_to_all.64 = f32[32,2,1536]{2,1,0:T(2,128)S(1)} all-to-all(f32[32,2,1536]{2,1,0:T(2,128)S(1)} %broadcast_in_dim.162), channel_id=1, replica_groups=mesh['noise'=8,'dp'=32] {'dp'}, dimensions={0} | all-to-all | bytes 786432 | tf_op jit(solution)/shard_map/all_to_all | solution.py:15
  111.0 0.3 fusion.58
  111.3 0.7 slice.455
  112.0 0.7 slice.456
  112.8 1.0 multiply_add_fusion.2
  114.3 0.5 fusion.13
  114.8 0.7 exponential_reduce_fusion.3
  115.5 9.0 %all_to_all.65 = f32[8,2,384]{2,1,0:T(2,128)S(1)} all-to-all(f32[8,2,384]{2,1,0:T(2,128)S(1)} %broadcast_in_dim.163), channel_id=1, replica_groups=mesh['noise'=8,'dp'=32] {'noise'}, dimensions={0} | all-to-all | bytes 49152 | tf_op jit(solution)/shard_map/all_to_all | solution.py:15
  124.8 0.5 fusion.14
  125.3 0.7 exponential_reduce_fusion.2
  126.1 0.1 broadcast_in_dim.164
  126.2 14.9 %all_to_all.66 = f32[32,2,1536]{2,1,0:T(2,128)S(1)} all-to-all(f32[32,2,1536]{2,1,0:T(2,128)S(1)} %broadcast_in_dim.164), channel_id=1, replica_groups=mesh['noise'=8,'dp'=32] {'dp'}, dimensions={0} | all-to-all | bytes 786432 | tf_op jit(solution)/shard_map/all_to_all | solution.py:15
  141.1 0.3 fusion.57
  141.4 0.7 slice.491
  142.1 0.7 slice.492
  142.8 1.0 multiply_add_fusion.1
  144.4 0.5 fusion.15
  144.8 0.7 exponential_reduce_fusion.1
  145.6 9.0 %all_to_all.67 = f32[8,2,384]{2,1,0:T(2,128)S(1)} all-to-all(f32[8,2,384]{2,1,0:T(2,128)S(1)} %broadcast_in_dim.165), channel_id=1, replica_groups=mesh['noise'=8,'dp'=32] {'noise'}, dimensions={0} | all-to-all | bytes 49152 | tf_op jit(solution)/shard_map/all_to_all | solution.py:15
  154.9 0.6 select_reduce_fusion
  155.5 0.5 fusion.17
  156.0 0.7 exponential_reduce_fusion
  156.7 0.8 broadcast_in_dim.167
  157.6 4.8 %all-to-all-start.9 = ((f32[32,2,1536]{2,1,0:T(2,128)}), f32[32,2,1536]{2,1,0:T(2,128)S(1)}, u32[]{:S(2)}, u32[]{:S(2)}) async-start(f32[32,2,1536]{2,1,0:T(2,128)} %broadcast_in_dim.167), calls=%async_computation.9 | async-start | bytes 786432 | tf_op jit(solution)/shard_map/all_to_all | solution.py:15
  162.4 7.4 %fusion.16 = f32[512,384]{0,1:T(8,128)} fusion(f32[1536,512]{1,0:T(8,128)} %param.4, f32[1536,384]{0,1:T(8,128)S(1)} %get-tuple-element.65, f32[384]{0:T(512)} %copy-done.1, f32[1536]{0:T(1024)S(1)} %fusion.34, f32[]{:T(128)S(6)} %neg.7, pred[1536]{0:T(1024)(128)(4,1)S(1)} %iota_compare_fusion, pred[384]{0:T(512)(128)(4,1)S(1)} %iota_compare_fusion.1), kind=kOutput, calls=%fused_computation.34 | convolution fusion | flops 3627417600 | bytes 6301060 | tf_op jit(solution)/shard_map/dot_general | solution.py:176
  169.8 2.3 copy.61
  172.1 0.6 all-to-all-done.9
  172.7 4.2 %all-to-all-start.11 = ((f32[8,64,384]{2,1,0:T(8,128)}), f32[8,64,384]{2,1,0:T(8,128)}, u32[]{:S(2)}, u32[]{:S(2)}) async-start(f32[8,64,384]{2,1,0:T(8,128)} %bitcast.63), calls=%async_computation.11 | async-start | bytes 1572864 | tf_op jit(solution)/shard_map/all_to_all | solution.py:88
  176.9 1.0 fusion.56
  178.0 0.9 copy.97
  179.0 0.7 slice.538
  179.6 0.7 slice.539
  180.3 1.0 multiply_add_fusion
  181.8 7.6 %fusion.1 = f32[1536,512]{0,1:T(8,128)} fusion(f32[384,512]{0,1:T(8,128)S(1)} %bitcast.62, f32[1536,384]{0,1:T(8,128)S(1)} %get-tuple-element.65, f32[1536]{0:T(1024)S(1)} %add_reduce_fusion, f32[384]{0:T(512)S(1)} %copy-done.2, f32[]{:T(128)S(6)} %neg.6, pred[1536]{0:T(1024)(128)(4,1)S(1)} %iota_compare_fusion, pred[384]{0:T(512)(128)(4,1)S(1)} %iota_compare_fusion.1), kind=kOutput, calls=%fused_computation.5 | convolution fusion | flops 3628007424 | bytes 6301060 | tf_op jit(solution)/shard_map/dot_general | solution.py:164
  189.4 11.2 %all-to-all-done.11 = f32[8,64,384]{2,1,0:T(8,128)} async-done(((f32[8,64,384]{2,1,0:T(8,128)}), f32[8,64,384]{2,1,0:T(8,128)}, u32[]{:S(2)}, u32[]{:S(2)}) %all-to-all-start.11) | async-done | bytes 786464 | tf_op jit(solution)/shard_map/all_to_all | solution.py:88
  200.6 7.0 %all-to-all-start.10 = ((f32[32,16,1536]{2,1,0:T(8,128)}), f32[32,16,1536]{2,1,0:T(8,128)S(1)}, u32[]{:S(2)}, u32[]{:S(2)}) async-start(f32[32,16,1536]{2,1,0:T(8,128)} %bitcast.60), calls=%async_computation.10 | async-start | bytes 6291456 | tf_op jit(solution)/shard_map/all_to_all | solution.py:88
  207.6 0.6 broadcast_select_fusion
  208.2 1.8 reduce_sum.129
  210.0 37.3 %all-to-all-done.10 = f32[32,16,1536]{2,1,0:T(8,128)S(1)} async-done(((f32[32,16,1536]{2,1,0:T(8,128)}), f32[32,16,1536]{2,1,0:T(8,128)S(1)}, u32[]{:S(2)}, u32[]{:S(2)}) %all-to-all-start.10) | async-done | bytes 3145760 | tf_op jit(solution)/shard_map/all_to_all | solution.py:88
  247.3 0.8 reduce_sum.128
  (159 shorter events, 3.3 us)
Async XLA Ops:
  18.5 31.8 %all-to-all-start = ((f32[8,384,64]{1,2,0:T(8,128)}), f32[8,384,64]{1,2,0:T(8,128)S(1)}, u32[]{:S(2)}, u32[]{:S(2)}) async-start(f32[8,384,64]{1,2,0:T(8,128)} %broadcast_in_dim.84), calls=%async_computation | async-start | bytes 1572864 | tf_op jit(solution)/shard_map/all_to_all | solution.py:15
  50.8 10.4 %all-to-all-start.3 = ((f32[8,1,1]{2,1,0:T(1,128)}), f32[8,1,1]{2,1,0:T(1,128)S(1)}, u32[]{:S(2)}, u32[]{:S(2)}) async-start(f32[8,1,1]{2,1,0:T(1,128)} %broadcast_in_dim.159), calls=%async_computation.3 | async-start | bytes 8192 | tf_op jit(solution)/shard_map/all_to_all | solution.py:15
  62.1 14.8 %all-to-all-start.2 = ((f32[32,2,1536]{2,1,0:T(2,128)}), f32[32,2,1536]{2,1,0:T(2,128)S(1)}, u32[]{:S(2)}, u32[]{:S(2)}) async-start(f32[32,2,1536]{2,1,0:T(2,128)} %broadcast_in_dim.156), calls=%async_computation.2 | async-start | bytes 786432 | tf_op jit(solution)/shard_map/all_to_all | solution.py:15
  144.3 18.1 %copy-start = (f32[1536]{0:T(1024)}, f32[1536]{0:T(1024)S(1)}, u32[]{:S(2)}) copy-start(f32[1536]{0:T(1024)S(1)} %fusion.34) | copy-start | bytes 18436
  155.5 1.2 copy-start.1
  157.6 15.1 %all-to-all-start.9 = ((f32[32,2,1536]{2,1,0:T(2,128)}), f32[32,2,1536]{2,1,0:T(2,128)S(1)}, u32[]{:S(2)}, u32[]{:S(2)}) async-start(f32[32,2,1536]{2,1,0:T(2,128)} %broadcast_in_dim.167), calls=%async_computation.9 | async-start | bytes 786432 | tf_op jit(solution)/shard_map/all_to_all | solution.py:15
  172.7 27.9 %all-to-all-start.11 = ((f32[8,64,384]{2,1,0:T(8,128)}), f32[8,64,384]{2,1,0:T(8,128)}, u32[]{:S(2)}, u32[]{:S(2)}) async-start(f32[8,64,384]{2,1,0:T(8,128)} %bitcast.63), calls=%async_computation.11 | async-start | bytes 1572864 | tf_op jit(solution)/shard_map/all_to_all | solution.py:88
  176.9 4.8 %copy-start.2 = (f32[384]{0:T(512)S(1)}, f32[384]{0:T(512)}, u32[]{:S(2)}) copy-start(f32[384]{0:T(512)} %copy-done.1) | copy-start | bytes 4612
  200.6 7.0 %copy-start.3 = (f32[384]{0:T(512)S(1)}, f32[384]{0:T(512)}, u32[]{:S(2)}) copy-start(f32[384]{0:T(512)} %get-tuple-element.5) | copy-start | bytes 4612
  200.6 46.7 %all-to-all-start.10 = ((f32[32,16,1536]{2,1,0:T(8,128)}), f32[32,16,1536]{2,1,0:T(8,128)S(1)}, u32[]{:S(2)}, u32[]{:S(2)}) async-start(f32[32,16,1536]{2,1,0:T(8,128)} %bitcast.60), calls=%async_computation.10 | async-start | bytes 6291456 | tf_op jit(solution)/shard_map/all_to_all | solution.py:88
where the time goes:
time: 249 us; the launch traced here: 248 us
  waiting for transfers between devices  77.6 us (31%)
  blocking collectives  76.2 us (31%)
  starting transfers between devices  31.9 us (13%)
  matrix products  21.3 us (9%)
  other arithmetic  19.8 us (8%)
  local copies, waits for them, and re-layouts  17.1 us (7%)
  between operations  4.09 us (2%)
    all_to_all x6, blocking collectives, from_everyone(): lax.all_to_all(jnp.broadcast_to(shard[None], (devices, *shard.shape)), ax...  76.2 us
    all_to_all x2, waiting for transfers between devices, sent_and_summed(): lax.all_to_all(in_blocks(shard, dim, devices), axis, 0, 0, tiled=True)  48.5 us
    all_to_all x4, waiting for transfers between devices, from_everyone(): lax.all_to_all(jnp.broadcast_to(shard[None], (devices, *shard.shape)), ax...  29.1 us
    all_to_all x4, starting transfers between devices, from_everyone(): lax.all_to_all(jnp.broadcast_to(shard[None], (devices, *shard.shape)), ax...  20.8 us
    all_to_all x2, starting transfers between devices, sent_and_summed(): lax.all_to_all(in_blocks(shard, dim, devices), axis, 0, 0, tiled=True)  11.2 us
    dot_general x1, matrix products, on_device(): lax.dot_general(coords, noise_weights, (((0,), (1,)), ((), ())), precisio...  7.61 us
    slice x88, local copies, waits for them, and re-layouts, combined_pairwise(): part[side::2]  7.42 us
    dot_general x1, matrix products, on_device(): lax.dot_general(coords, data_weights, (((0,), (0,)), ((), ())), precision...  7.38 us
  transfers between devices with their start and end apart: 6, of which 5 were waited for; matrix products, arithmetic and copies ran while one was open for 14% of the time, Pallas kernels for 0%

commit v1 on v0

v1 whole, which is shorter than its diff:
```python
import jax
import jax.numpy as jnp
from jax import lax
from jax.experimental import pallas as pl
from jax.experimental.pallas import tpu as pltpu
from jax.sharding import Mesh, PartitionSpec as P


BLOCK = 128
ITERS = 3
SMOOTHING_TEMP = 0.125
SHARP = 1.0 / SMOOTHING_TEMP

F32 = jnp.float32
BF16 = jnp.bfloat16
NZ, NXY, NC = 8, 16, 2
ROWS, COLS, DIM = 1536, 384, 512
RB, CB = ROWS // BLOCK, COLS // BLOCK
CHUNK = DIM // NZ
OWN = DIM // (NXY * NC)
LROWS = 16
TOPS = RB * OWN
LEVELS = TOPS + RB
PIECE = TOPS + 2 * RB

SMEM = pl.BlockSpec(memory_space=pltpu.SMEM)
VMEM = pl.BlockSpec(memory_space=pltpu.VMEM)


def shaped(shape, dtype=F32):
    return jax.ShapeDtypeStruct(shape, dtype)


def call(body, outs, ins, scratch=(), limit=16):
    return pl.pallas_call(
        body,
        out_shape=outs,
        in_specs=ins,
        out_specs=jax.tree.map(lambda _: VMEM, outs),
        scratch_shapes=scratch,
        cost_estimate=pl.CostEstimate(flops=1000000, transcendentals=0, bytes_accessed=4000000),
        compiler_params=pltpu.CompilerParams(vmem_limit_bytes=limit << 20),
    )


def halves(value):
    high = value.astype(BF16)
    return high, (value - high.astype(F32)).astype(BF16)


def dot(a, b, dims):
    return lax.dot_general(a, b, (dims, ((), ())), preferred_element_type=F32)


def dot3(a, b, dims):
    return dot(a[0], b[0], dims) + (dot(a[0], b[1], dims) + dot(a[1], b[0], dims))


def diagonal():
    return lax.broadcasted_iota(jnp.int32, (BLOCK, BLOCK), 0) == lax.broadcasted_iota(
        jnp.int32, (BLOCK, BLOCK), 1
    )


def to_row(column, eye):
    return jnp.sum(jnp.where(eye, column, 0.0), axis=0, keepdims=True)


def to_column(row, eye):
    return jnp.sum(jnp.where(eye, jnp.broadcast_to(row, (BLOCK, BLOCK)), 0.0), axis=1, keepdims=True)


def prepare_body(points, high, low, turned_high, turned_low, squares):
    for k in range(0, ROWS, 256):
        part = points[k : k + 256, :]
        squares[k : k + 256, :] = jnp.sum(part * part, axis=1, keepdims=True)
        a, b = halves(part)
        high[k : k + 256, :] = a
        low[k : k + 256, :] = b
        a, b = halves(part.T)
        turned_high[:, k : k + 256] = a
        turned_low[:, k : k + 256] = b


def row_lse(cost, bias, k):
    scores = bias - cost[k * BLOCK : (k + 1) * BLOCK, :]
    top = jnp.max(scores, axis=1, keepdims=True)
    return top + jnp.log(jnp.sum(jnp.exp(scores - top), axis=1, keepdims=True))


def live_columns(info):
    return lax.broadcasted_iota(jnp.int32, (1, COLS), 1) < info[3] * BLOCK


def store_count(out, row, count):
    out[row : row + 1, :] = jnp.full((1, BLOCK), (count * BLOCK).astype(F32))


def cost_body(info, high, low, squares, *refs):
    pieces, (cost, out, turned, data_high, data_low) = refs[:NZ], refs[NZ:]
    square = jnp.zeros((1, COLS), F32)
    for s in range(NZ):
        z = lax.rem(info[0] + (NZ - s), NZ)
        piece = pieces[s][...]
        square += jnp.sum(piece * piece, axis=0, keepdims=True)
        a, b = halves(piece)
        at = pl.multiple_of(z * CHUNK, CHUNK)
        data_high[pl.ds(at, CHUNK), :] = a
        data_low[pl.ds(at, CHUNK), :] = b
        for q in range(CHUNK // OWN):
            to = pl.multiple_of((z * 2 + q // 2) * OWN, OWN)
            turned[q % 2, 0, pl.ds(to, OWN), :] = a[q * OWN : (q + 1) * OWN]
            turned[q % 2, 1, pl.ds(to, OWN), :] = b[q * OWN : (q + 1) * OWN]
    eye = diagonal()
    bias = jnp.where(live_columns(info), 0.0, -jnp.inf)
    both = (data_high[...], data_low[...])
    for k in range(0, ROWS, 256):
        cross = dot3((high[k : k + 256, :], low[k : k + 256, :]), both, ((1,), (0,)))
        cost[k : k + 256, :] = SHARP * (squares[k : k + 256, :] + square - 2.0 * cross)
    out[...] = jnp.zeros((LROWS, BLOCK), F32)
    for k in range(RB):
        out[k : k + 1, :] = to_row(row_lse(cost, bias, k), eye)
    store_count(out, RB, info[3])


def joined(values):
    top = jnp.max(values, axis=0)
    return top + jnp.log(jnp.sum(jnp.exp(values - top[None]), axis=0))


def column_bias(got, info):
    values = got[...]
    total = jnp.sum(values[:, CB, :], axis=0, keepdims=True)
    level = joined(values)
    parts = [-(level[k : k + 1, :] - jnp.log(total)) for k in range(CB)]
    return jnp.where(live_columns(info), jnp.concatenate(parts, axis=1), -jnp.inf)


def row_body(info, got, cost, out):
    bias = column_bias(got, info)
    eye = diagonal()
    out[...] = jnp.zeros((LROWS, BLOCK), F32)
    for k in range(RB):
        out[k : k + 1, :] = to_row(row_lse(cost, bias, k), eye)
    store_count(out, RB, info[3])


def column_body(info, got, cost, out, dual, column):
    values = got[...]
    total = jnp.sum(values[:, RB, :], axis=0, keepdims=True)
    duals = -(joined(values) - jnp.log(total))
    dual[...] = duals
    eye = diagonal()
    tops = []
    for k in range(RB):
        row = jnp.where(k < info[2], duals[k : k + 1, :], -jnp.inf)
        bias = to_column(row, eye)
        column[k * BLOCK : (k + 1) * BLOCK, :] = bias
        scores = bias - cost[k * BLOCK : (k + 1) * BLOCK, :]
        tops.append(jnp.max(scores.reshape(BLOCK // 8, 8, COLS), axis=0))
    top = tops[0]
    for k in range(1, RB):
        top = jnp.maximum(top, tops[k])
    top = jnp.max(top, axis=0, keepdims=True)
    mass = jnp.zeros((8, COLS), F32)
    for k in range(RB):
        part = slice(k * BLOCK, (k + 1) * BLOCK)
        scores = jnp.exp(column[part, :] - cost[part, :] - top)
        mass += jnp.sum(scores.reshape(BLOCK // 8, 8, COLS), axis=0)
    level = top + jnp.log(jnp.sum(mass, axis=0, keepdims=True))
    value = jnp.concatenate(
        [level[:, k * BLOCK : (k + 1) * BLOCK] for k in range(CB)]
        + [jnp.full((1, BLOCK), (info[2] * BLOCK).astype(F32))]
        + [jnp.zeros((8 - CB - 1, BLOCK), F32)],
        axis=0,
    )
    for z in range(NZ):
        out[z] = value


def project_noise_body(own, column, cost, turned_high, turned_low, out, weights_high, weights_low):
    level = jnp.concatenate([own[0, k : k + 1, :] for k in range(CB)], axis=1)
    for k in range(0, ROWS, 256):
        part = slice(k, k + 256)
        a, b = halves(jnp.exp(column[part, :] - cost[part, :] - level))
        weights_high[part, :] = a
        weights_low[part, :] = b
    both = (weights_high[...], weights_low[...])
    for k in range(0, DIM, 256):
        some = dot3((turned_high[k : k + 256, :], turned_low[k : k + 256, :]), both, ((1,), (0,)))
        for q in range(256 // CHUNK):
            for c in range(CB):
                out[k // CHUNK + q, c * CHUNK : (c + 1) * CHUNK, :] = some[
                    q * CHUNK : (q + 1) * CHUNK, c * BLOCK : (c + 1) * BLOCK
                ]


def spread(out, some, k):
    for p in range(NXY):
        for h in range(2):
            out[p, (k * 2 + h) * OWN : (k * 2 + h + 1) * OWN, :] = some[
                p * OWN : (p + 1) * OWN, h * BLOCK : (h + 1) * BLOCK
            ]


def project_data_body(info, got, cost, turned, out, high, low, dual, tops):
    bias = column_bias(got, info)
    dual[...] = bias
    eye = diagonal()
    for k in range(RB):
        part = slice(k * BLOCK, (k + 1) * BLOCK)
        scores = bias - cost[part, :]
        top = jnp.max(scores, axis=1, keepdims=True)
        weights = jnp.exp(scores - top)
        level = top + jnp.log(jnp.sum(weights, axis=1, keepdims=True))
        tops[k : k + 1, :] = to_row(top, eye)
        tops[RB + k : RB + k + 1, :] = to_row(level, eye)
        a, b = halves(weights)
        high[part, :] = a
        low[part, :] = b
    other = 1 - info[1]
    for k in range(ROWS // 256):
        part = slice(k * 256, (k + 1) * 256)
        some = dot3((turned[other, 0], turned[other, 1]), (high[part, :], low[part, :]), ((1,), (1,)))
        spread(out, some, k)
    for p in range(NXY):
        out[p, TOPS:PIECE, :] = tops[...]


def project_own_body(info, turned, high, low, out):
    mine = info[1]
    for k in range(ROWS // 256):
        part = slice(k * 256, (k + 1) * 256)
        some = dot3((turned[mine, 0], turned[mine, 1]), (high[part, :], low[part, :]), ((1,), (1,)))
        spread(out, some, k)


def merge_body(own, own_tops, came, out):
    a, b = own_tops[RB : 2 * RB, :], came[0, LEVELS:PIECE, :]
    top = jnp.maximum(a, b)
    level = top + jnp.log(jnp.exp(a - top) + jnp.exp(b - top))
    a, b = jnp.exp(own_tops[0:RB, :] - level), jnp.exp(came[0, TOPS:LEVELS, :] - level)
    for k in range(RB):
        part = slice(k * OWN, (k + 1) * OWN)
        out[:, part, :] = (
            own[:, part, :] * a[k : k + 1, :][None] + came[:, part, :] * b[k : k + 1, :][None]
        )
    for p in range(NXY):
        out[p, LEVELS:PIECE, :] = level
        out[p, TOPS:LEVELS, :] = level


def finish_noise_body(info, came, out):
    levels = came[:, LEVELS:PIECE, :]
    shares = jnp.exp(levels - joined(levels)[None])
    for k in range(RB):
        part = slice(k * OWN, (k + 1) * OWN)
        total = jnp.sum(came[:, part, :] * shares[:, k : k + 1, :], axis=0)
        out[:, k * BLOCK : (k + 1) * BLOCK] = jnp.where(k < info[2], total, 0.0)


def finish_data_body(info, came, got, out):
    levels = got[...]
    shares = jnp.exp(levels - joined(levels)[None])
    for k in range(CB):
        part = slice(k * CHUNK, (k + 1) * CHUNK)
        total = jnp.sum(came[:, part, :] * shares[:, k : k + 1, :], axis=0)
        out[:, k * BLOCK : (k + 1) * BLOCK] = jnp.where(k < info[3], total, 0.0)


CORES = [(0, 1), (1, 0)]


def over_dp(lse):
    came = lax.ppermute(lse, "c", CORES)
    top = jnp.maximum(lse, came)
    both = top + jnp.log(jnp.exp(lse - top) + jnp.exp(came - top))
    counts = lax.broadcasted_iota(jnp.int32, (LROWS, BLOCK), 0) == RB
    both = jnp.where(counts, lse + came, both)
    return lax.all_to_all(
        jnp.broadcast_to(both[None], (NXY, LROWS, BLOCK)), ("x", "y"), 0, 0, tiled=True
    )


def over_noise(pieces):
    return lax.all_to_all(pieces, "z", 0, 0, tiled=True)


def on_device(noise_points, data_points, noise_blocks, data_blocks):
    info = jnp.concatenate(
        [lax.axis_index("z").reshape(1), lax.axis_index("c").reshape(1), noise_blocks, data_blocks]
    )
    mine = data_points.T
    pieces = [mine] + [
        lax.ppermute(mine, "z", [(i, (i + s) % NZ) for i in range(NZ)]) for s in range(1, NZ)
    ]
    high, low, turned_high, turned_low, squares = call(
        prepare_body,
        (
            shaped((ROWS, DIM), BF16),
            shaped((ROWS, DIM), BF16),
            shaped((DIM, ROWS), BF16),
            shaped((DIM, ROWS), BF16),
            shaped((ROWS, 1)),
        ),
        [VMEM],
    )(noise_points)
    cost, lse, turned = call(
        cost_body,
        (shaped((ROWS, COLS)), shaped((LROWS, BLOCK)), shaped((NC, 2, DIM // NC, COLS), BF16)),
        [SMEM] + [VMEM] * (3 + NZ),
        [pltpu.VMEM((DIM, COLS), BF16), pltpu.VMEM((DIM, COLS), BF16)],
    )(info, high, low, squares, *pieces)
    for turn in range(ITERS):
        if turn:
            lse = call(row_body, shaped((LROWS, BLOCK)), [SMEM, VMEM, VMEM])(info, got, cost)
        rows = over_dp(lse)
        sent, dual, column = call(
            column_body,
            (shaped((NZ, 8, BLOCK)), shaped((LROWS, BLOCK)), shaped((ROWS, 1))),
            [SMEM, VMEM, VMEM],
        )(info, rows, cost)
        got = over_noise(sent)
    halfway = call(
        project_noise_body,
        shaped((NZ, CB * CHUNK, BLOCK)),
        [VMEM] * 5,
        [pltpu.VMEM((ROWS, COLS), BF16), pltpu.VMEM((ROWS, COLS), BF16)],
    )(sent, column, cost, turned_high, turned_low)
    got, halfway = lax.optimization_barrier((got, halfway))
    data_came = over_noise(halfway)
    theirs, weights_high, weights_low, data_dual, level = call(
        project_data_body,
        (
            shaped((NXY, PIECE, BLOCK)),
            shaped((ROWS, COLS), BF16),
            shaped((ROWS, COLS), BF16),
            shaped((1, COLS)),
            shaped((2 * RB, BLOCK)),
        ),
        [SMEM, VMEM, VMEM, VMEM],
    )(info, got, cost, turned)
    came = lax.ppermute(theirs, "c", CORES)
    own = call(
        project_own_body, shaped((NXY, RB * OWN, BLOCK)), [SMEM, VMEM, VMEM, VMEM]
    )(info, turned, weights_high, weights_low)
    merged = call(merge_body, shaped((NXY, PIECE, BLOCK)), [VMEM] * 3)(own, level, came)
    noise_came = lax.all_to_all(merged, ("x", "y"), 0, 0, tiled=True)
    noise_target = call(finish_noise_body, shaped((OWN, ROWS)), [SMEM, VMEM])(info, noise_came)
    data_target = call(
        finish_data_body, shaped((CHUNK, COLS)), [SMEM, VMEM, VMEM]
    )(info, data_came, got)
    row_live = jnp.arange(ROWS, dtype=jnp.int32) < noise_blocks[0] * BLOCK
    column_live = jnp.arange(COLS, dtype=jnp.int32) < data_blocks[0] * BLOCK
    noise_potential = jnp.where(row_live, SMOOTHING_TEMP * dual[:RB].reshape(ROWS), 0.0)
    data_potential = jnp.where(column_live, SMOOTHING_TEMP * data_dual.reshape(COLS), 0.0)
    return noise_potential, data_potential, noise_target, data_target


def solution(mesh):
    axes = Mesh(mesh.devices.reshape(NZ, 4, 4, NC), ("z", "x", "y", "c"))
    dp = ("x", "y", "c")
    return jax.shard_map(
        on_device,
        mesh=axes,
        in_specs=(P("z", None), P(dp, "z"), P("z"), P(dp)),
        out_specs=(P("z"), P(dp), P(dp, "z"), P("z", dp)),
        check_vma=False,
    )
```

time: 249 us -> 190 us (0.76)
  Pallas kernels: 0 us -> 29.8 us
  waiting for transfers between devices: 77.6 us -> 47.8 us
  blocking collectives: 76.2 us -> 52.1 us
  matrix products: 21.3 us -> 0 us
  other arithmetic: 19.8 us -> 1.49 us
  starting transfers between devices: 31.9 us -> 41.4 us
    all_to_all x6 -> x3, waiting for transfers between devices: 77.6 us -> 39.4 us  [the longest x1 22 us: on_device(): noise_came = lax.all_to_all(merged, ('x', 'y'), 0, 0, tiled=True)]
    pallas_call x0 -> x13, Pallas kernels: none -> 29.8 us  [the longest x3 5.48 us: on_device(): call(column_body, (shaped((NZ, 8, BLOCK)), shaped((LROWS, BLOCK)), shaped...]
    ppermute x0 -> x11, starting transfers between devices: none -> 27.6 us  [the longest x7 17.4 us: on_device(): lax.ppermute(mine, 'z', [(i, (i + s) % NZ) for i in range(NZ)])]
    all_to_all x6 -> x5, blocking collectives: 76.2 us -> 52.1 us  [the longest x3 32.9 us: over_dp(): lax.all_to_all(jnp.broadcast_to(both[None], (NXY, LROWS, BLOCK)), ('x', '...]
    dot_general x3 -> x0, matrix products: 21.3 us -> none  [the longest x1 7.61 us: on_device(): lax.dot_general(coords, noise_weights, (((0,), (1,)), ((), ())), precisio...]
    all_to_all x6 -> x3, starting transfers between devices: 31.9 us -> 13.9 us  [the longest x2 10.2 us: over_noise(): return lax.all_to_all(pieces, 'z', 0, 0, tiled=True)]
    unnamed x20 -> x32, local copies, waits for them, and re-layouts: 1.05 us -> 14.7 us
    reduce_sum x13 -> x0, other arithmetic: 11 us -> none  [the longest x4 2.76 us: row_threshold(): mass = jnp.sum(jnp.exp(pair_scores - local[:, None]), axis=1)]
  transfers between devices with their start and end apart: 6 -> 14, of which waited for: 5 -> 6; matrix products, arithmetic and copies ran while one was open for 14% -> 1% of each run, Pallas kernels for 0% -> 7%
where the time goes in v1:
time: 190 us
  blocking collectives  52.1 us (27%)
  waiting for transfers between devices  47.8 us (25%)
  starting transfers between devices  41.4 us (22%)
  Pallas kernels  29.8 us (16%)
  local copies, waits for them, and re-layouts  14.8 us (8%)
  between operations  2.1 us (1%)
    all_to_all x3, blocking collectives, over_dp(): lax.all_to_all(jnp.broadcast_to(both[None], (NXY, LROWS, BLOCK)), ('x', '...  32.9 us
    all_to_all x1, waiting for transfers between devices, on_device(): noise_came = lax.all_to_all(merged, ('x', 'y'), 0, 0, tiled=True)  22 us
    all_to_all x2, blocking collectives, over_noise(): return lax.all_to_all(pieces, 'z', 0, 0, tiled=True)  19.2 us
    all_to_all x2, waiting for transfers between devices, over_noise(): return lax.all_to_all(pieces, 'z', 0, 0, tiled=True)  17.4 us
    ppermute x7, starting transfers between devices, on_device(): lax.ppermute(mine, 'z', [(i, (i + s) % NZ) for i in range(NZ)])  17.4 us
    unnamed x32, local copies, waits for them, and re-layouts  14.7 us
    all_to_all x2, starting transfers between devices, over_noise(): return lax.all_to_all(pieces, 'z', 0, 0, tiled=True)  10.2 us
    ppermute x3, starting transfers between devices, over_dp(): came = lax.ppermute(lse, 'c', CORES)  8.39 us
  transfers between devices with their start and end apart: 14, of which 6 were waited for; matrix products, arithmetic and copies ran while one was open for 1% of the time, Pallas kernels for 7%

profile of v1, /device:TPU:1, one launch (start us, length us, event | category | flops | bytes accessed | tf_op | source)
XLA Modules:
  0.0 189.5 jit_solution(15650469117951397039)
XLA Ops:
  0.6 2.5 %collective-permute-start = (f32[64,384]{1,0:T(8,128)}, f32[64,384]{1,0:T(8,128)S(1)}, u32[]{:S(2)}, u32[]{:S(2)}) collective-permute-start(f32[64,384]{1,0:T(8,128)} %bitcast.7), channel_id=1, source_target_pairs={{0,32},{32,64},{64,96},{96,128},{128,160},{160,192},{192,224},{224... | collective-permute-start | bytes 294920 | tf_op jit(solution)/shard_map/ppermute | solution.py:295
  3.2 3.0 %collective-permute-start.1 = (f32[64,384]{1,0:T(8,128)}, f32[64,384]{1,0:T(8,128)S(1)}, u32[]{:S(2)}, u32[]{:S(2)}) collective-permute-start(f32[64,384]{1,0:T(8,128)} %bitcast.8), channel_id=1, source_target_pairs={{0,64},{32,96},{64,128},{96,160},{128,192},{160,224},{192,0},{224,... | collective-permute-start | bytes 294920 | tf_op jit(solution)/shard_map/ppermute | solution.py:295
  6.2 3.8 %collective-permute-start.2 = (f32[64,384]{1,0:T(8,128)}, f32[64,384]{1,0:T(8,128)S(1)}, u32[]{:S(2)}, u32[]{:S(2)}) collective-permute-start(f32[64,384]{1,0:T(8,128)} %bitcast.9), channel_id=1, source_target_pairs={{0,96},{32,128},{64,160},{96,192},{128,224},{160,0},{192,32},{224,... | collective-permute-start | bytes 294920 | tf_op jit(solution)/shard_map/ppermute | solution.py:295
  9.9 0.5 collective-permute-start.3
  10.4 4.5 %collective-permute-start.4 = (f32[64,384]{1,0:T(8,128)}, f32[64,384]{1,0:T(8,128)S(1)}, u32[]{:S(2)}, u32[]{:S(2)}) collective-permute-start(f32[64,384]{1,0:T(8,128)} %bitcast.11), channel_id=1, source_target_pairs={{0,160},{32,192},{64,224},{96,0},{128,32},{160,64},{192,96},{224,1... | collective-permute-start | bytes 294920 | tf_op jit(solution)/shard_map/ppermute | solution.py:295
  16.1 1.9 copy-done
  18.0 1.5 shard_map.75
  19.5 1.2 copy-done.3
  20.7 0.0 collective-permute-done.refs_1_
  20.7 2.5 %collective-permute-start.5 = (f32[64,384]{1,0:T(8,128)S(1)}, f32[64,384]{1,0:T(8,128)S(1)}, u32[]{:S(2)}, u32[]{:S(2)}) collective-permute-start(f32[64,384]{1,0:T(8,128)S(1)} %bitcast.12), channel_id=1, source_target_pairs={{0,192},{32,224},{64,0},{96,32},{128,64},{160,96},{192,128},{224,1... | collective-permute-start | bytes 294920 | tf_op jit(solution)/shard_map/ppermute | solution.py:295
  23.1 0.0 collective-permute-done.1.refs_2_
  23.1 0.7 collective-permute-start.6
  23.9 0.1 pad_add_fusion.info
  24.0 0.0 collective-permute-done.2.refs_3_
  24.0 0.0 collective-permute-done.3.refs_4_
  24.0 0.0 collective-permute-done.4.refs_5_
  24.0 0.0 copy-start.14
  24.0 0.6 copy-done.14
  24.6 5.9 %collective-permute-done.5.refs_6_ = f32[64,384]{1,0:T(8,128)S(1)} collective-permute-done((f32[64,384]{1,0:T(8,128)S(1)}, f32[64,384]{1,0:T(8,128)S(1)}, u32[]{:S(2)}, u32[]{:S(2)}) %collective-permute-start.5) | collective-permute-done | bytes 98336 | tf_op jit(solution)/shard_map/ppermute | solution.py:295
  30.5 0.9 copy-done.15
  31.4 3.6 %shard_map.76 = (f32[1536,384]{1,0:T(8,128)S(1)}, f32[16,128]{1,0:T(8,128)S(1)}, bf16[2,2,256,384]{3,2,1,0:T(8,128)(2,1)S(1)}) custom-call(s32[4]{0:T(128)S(1)} %pad_add_fusion.info, bf16[1536,512]{1,0:T(8,128)(2,1)S(1)} %get-tuple-element.24.high, bf16[1536,512]{1,0:T(8,128)(2,1)S(1)} %get-tuple-element.25.low, f32[1536,1]{1,0:T(8,128)S(1)} %get-tuple-element.26.squares, ...), custom_call_target="tpu_custom_call" | custom-call | flops 1000000 | bytes 4000000 | tf_op jit(solution)/shard_map/pallas_call | solution.py:308
  35.1 2.1 %collective-permute-start.7 = (f32[16,128]{1,0:T(8,128)S(1)}, f32[16,128]{1,0:T(8,128)S(1)}, u32[]{:S(2)}, u32[]{:S(2)}) collective-permute-start(f32[16,128]{1,0:T(8,128)S(1)} %get-tuple-element.27), channel_id=1, source_target_pairs={{0,1},{1,0},{2,3},{3,2},{4,5},{5,4},{6,7},{7,6},{8,9},{9,8},{10,11... | collective-permute-start | bytes 24584 | tf_op jit(solution)/shard_map/ppermute | solution.py:275
  37.2 0.8 collective-permute-done.7
  38.0 0.1 add_select_fusion.2
  38.1 13.3 %all_to_all.40.got = f32[16,16,128]{2,1,0:T(8,128)S(1)} all-to-all(f32[16,16,128]{2,1,0:T(8,128)S(1)} %broadcast_in_dim.12), channel_id=1, replica_groups=mesh['z'=8,'x'=4,'y'=4,'c'=2] {'x','y'}, dimensions={0} | all-to-all | bytes 262144 | tf_op jit(solution)/shard_map/all_to_all | solution.py:280
  51.3 1.8 shard_map.77
  53.1 10.0 %all_to_all.41.got = f32[8,8,128]{2,1,0:T(8,128)S(1)} all-to-all(f32[8,8,128]{2,1,0:T(8,128)S(1)} %get-tuple-element.29), channel_id=1, replica_groups=mesh['z'=8,'x'=4,'y'=4,'c'=2] {'z'}, dimensions={0} | all-to-all | bytes 65536 | tf_op jit(solution)/shard_map/all_to_all | solution.py:286
  63.1 1.5 shard_map.78
  64.7 3.3 %collective-permute-start.8 = (f32[16,128]{1,0:T(8,128)S(1)}, f32[16,128]{1,0:T(8,128)S(1)}, u32[]{:S(2)}, u32[]{:S(2)}) collective-permute-start(f32[16,128]{1,0:T(8,128)S(1)} %shard_map.78), channel_id=1, source_target_pairs={{0,1},{1,0},{2,3},{3,2},{4,5},{5,4},{6,7},{7,6},{8,9},{9,8},{10,11... | collective-permute-start | bytes 24584 | tf_op jit(solution)/shard_map/ppermute | solution.py:275
  68.0 0.8 collective-permute-done.8
  68.8 0.1 add_select_fusion.1
  68.9 9.8 %all_to_all.42.got = f32[16,16,128]{2,1,0:T(8,128)S(1)} all-to-all(f32[16,16,128]{2,1,0:T(8,128)S(1)} %broadcast_in_dim.14), channel_id=1, replica_groups=mesh['z'=8,'x'=4,'y'=4,'c'=2] {'x','y'}, dimensions={0} | all-to-all | bytes 262144 | tf_op jit(solution)/shard_map/all_to_all | solution.py:280
  78.7 1.8 shard_map.79
  80.5 9.2 %all_to_all.43.got = f32[8,8,128]{2,1,0:T(8,128)S(1)} all-to-all(f32[8,8,128]{2,1,0:T(8,128)S(1)} %get-tuple-element.30), channel_id=1, replica_groups=mesh['z'=8,'x'=4,'y'=4,'c'=2] {'z'}, dimensions={0} | all-to-all | bytes 65536 | tf_op jit(solution)/shard_map/all_to_all | solution.py:286
  89.7 1.5 shard_map.80
  91.2 3.0 %collective-permute-start.9 = (f32[16,128]{1,0:T(8,128)S(1)}, f32[16,128]{1,0:T(8,128)S(1)}, u32[]{:S(2)}, u32[]{:S(2)}) collective-permute-start(f32[16,128]{1,0:T(8,128)S(1)} %shard_map.80), channel_id=1, source_target_pairs={{0,1},{1,0},{2,3},{3,2},{4,5},{5,4},{6,7},{7,6},{8,9},{9,8},{10,11... | collective-permute-start | bytes 24584 | tf_op jit(solution)/shard_map/ppermute | solution.py:275
  94.2 0.8 collective-permute-done.9
  95.1 0.1 add_select_fusion
  95.2 9.8 %all_to_all.44.got = f32[16,16,128]{2,1,0:T(8,128)S(1)} all-to-all(f32[16,16,128]{2,1,0:T(8,128)S(1)} %broadcast_in_dim.28), channel_id=1, replica_groups=mesh['z'=8,'x'=4,'y'=4,'c'=2] {'x','y'}, dimensions={0} | all-to-all | bytes 262144 | tf_op jit(solution)/shard_map/all_to_all | solution.py:280
  105.0 1.9 %shard_map.81 = (f32[8,8,128]{2,1,0:T(8,128)}, f32[16,128]{1,0:T(8,128)S(1)}, f32[1536,1]{1,0:T(8,128)S(1)}) custom-call(s32[4]{0:T(128)S(1)} %pad_add_fusion.info, f32[16,16,128]{2,1,0:T(8,128)S(1)} %all_to_all.44.got, f32[1536,384]{1,0:T(8,128)S(1)} %get-tuple-element.28.cost), custom_call_target="tpu_custom_call" | custom-call | flops 1000000 | bytes 4000000 | tf_op jit(solution)/shard_map/pallas_call | solution.py:318
  106.9 0.9 copy-done.11
  107.8 3.3 %all-to-all-start.5 = ((f32[8,8,128]{2,1,0:T(8,128)}), f32[8,8,128]{2,1,0:T(8,128)S(1)}, u32[]{:S(2)}, u32[]{:S(2)}) async-start(f32[8,8,128]{2,1,0:T(8,128)} %get-tuple-element.32.own), calls=%async_computation.5 | async-start | bytes 65536 | tf_op jit(solution)/shard_map/all_to_all | solution.py:286
  111.1 1.4 copy-done.4
  112.5 1.4 copy-done.6
  114.0 1.1 copy-done.12
  115.1 4.8 %shard_map.82 = f32[8,192,128]{2,1,0:T(8,128)} custom-call(f32[8,8,128]{2,1,0:T(8,128)} %get-tuple-element.32.own, f32[1536,1]{1,0:T(8,128)S(1)} %copy-done.12, f32[1536,384]{1,0:T(8,128)S(1)} %get-tuple-element.28.cost, bf16[512,1536]{1,0:T(8,128)(2,1)S(1)} %copy-done.4, bf16[512,1536]{1,0:T(8,128)(2,1)S(1)} %copy-done.6), custom_call_target="tpu_custom_call" | custom-call | flops 1000000 | bytes 4000000 | tf_op jit(solution)/shard_map/pallas_call | solution.py:324
  119.8 0.0 all-to-all-done.5.got
  119.9 3.7 %shard_map.83 = (f32[16,216,128]{2,1,0:T(8,128)}, bf16[1536,384]{1,0:T(8,128)(2,1)S(1)}, bf16[1536,384]{1,0:T(8,128)(2,1)S(1)}, f32[1,384]{1,0:T(1,128)S(1)}, f32[24,128]{1,0:T(8,128)S(1)}) custom-call(s32[4]{0:T(128)S(1)} %pad_add_fusion.info, f32[8,8,128]{2,1,0:T(8,128)S(1)} %all-to-all-done.5.got, f32[1536,384]{1,0:T(8,128)S(1)} %get-tuple-element.28.cost, ...), custom_call_target="tpu_custom_call" | custom-call | flops 1000000 | bytes 4000000 | tf_op jit(solution)/shard_map/pallas_call | solution.py:332
  123.6 1.0 copy-done.7
  124.6 1.0 copy-done.9
  125.6 1.8 collective-permute-start.10
  127.4 6.8 %all-to-all-start.7 = ((f32[8,192,128]{2,1,0:T(8,128)}), f32[8,192,128]{2,1,0:T(8,128)S(1)}, u32[]{:S(2)}, u32[]{:S(2)}) async-start(f32[8,192,128]{2,1,0:T(8,128)} %shard_map.82), calls=%async_computation.7 | async-start | bytes 1572864 | tf_op jit(solution)/shard_map/all_to_all | solution.py:286
  134.3 1.3 copy-done.10
  135.5 1.9 %shard_map.84.own = f32[16,192,128]{2,1,0:T(8,128)S(1)} custom-call(s32[4]{0:T(128)S(1)} %pad_add_fusion.info, bf16[2,2,256,384]{3,2,1,0:T(8,128)(2,1)S(1)} %get-tuple-element.37.turned, bf16[1536,384]{1,0:T(8,128)(2,1)S(1)} %copy-done.8, bf16[1536,384]{1,0:T(8,128)(2,1)S(1)} %copy-done.10), custom_call_target="tpu_custom_call" | custom-call | flops 1000000 | bytes 4000000 | tf_op jit(solution)/shard_map/pallas_call | solution.py:344
  137.5 3.0 %shard_map.85 = f32[16,216,128]{2,1,0:T(8,128)} custom-call(f32[16,192,128]{2,1,0:T(8,128)S(1)} %shard_map.84.own, f32[24,128]{1,0:T(8,128)S(1)} %get-tuple-element.41.own_tops, f32[16,216,128]{2,1,0:T(8,128)} %collective-permute-done.10.came), custom_call_target="tpu_custom_call" | custom-call | flops 1000000 | bytes 4000000 | tf_op jit(solution)/shard_map/pallas_call | solution.py:347
  140.5 17.4 %all-to-all-done.7.came = f32[8,192,128]{2,1,0:T(8,128)S(1)} async-done(((f32[8,192,128]{2,1,0:T(8,128)}), f32[8,192,128]{2,1,0:T(8,128)S(1)}, u32[]{:S(2)}, u32[]{:S(2)}) %all-to-all-start.7) | async-done | bytes 786464 | tf_op jit(solution)/shard_map/all_to_all | solution.py:286
  157.9 0.9 copy-done.1
  158.8 3.7 %all-to-all-start.6 = ((f32[16,216,128]{2,1,0:T(8,128)}), f32[16,216,128]{2,1,0:T(8,128)S(1)}, u32[]{:S(2)}, u32[]{:S(2)}) async-start(f32[16,216,128]{2,1,0:T(8,128)} %shard_map.85), calls=%async_computation.6 | async-start | bytes 3538944 | tf_op jit(solution)/shard_map/all_to_all | solution.py:348
  162.5 0.6 bitcast_select_fusion
  163.1 0.6 fusion.3
  163.7 1.1 copy-done.2
  164.8 1.3 shard_map.87
  166.1 22.0 %all-to-all-done.6.came = f32[16,216,128]{2,1,0:T(8,128)S(1)} async-done(((f32[16,216,128]{2,1,0:T(8,128)}), f32[16,216,128]{2,1,0:T(8,128)S(1)}, u32[]{:S(2)}, u32[]{:S(2)}) %all-to-all-start.6) | async-done | bytes 1769504 | tf_op jit(solution)/shard_map/all_to_all | solution.py:348
  188.1 1.4 shard_map.86
  (25 shorter events, 0.1 us)
Async XLA Ops:
  0.6 20.1 %collective-permute-start = (f32[64,384]{1,0:T(8,128)}, f32[64,384]{1,0:T(8,128)S(1)}, u32[]{:S(2)}, u32[]{:S(2)}) collective-permute-start(f32[64,384]{1,0:T(8,128)} %bitcast.7), channel_id=1, source_target_pairs={{0,32},{32,64},{64,96},{96,128},{128,160},{160,192},{192,224},{224... | collective-permute-start | bytes 294920 | tf_op jit(solution)/shard_map/ppermute | solution.py:295
  3.2 20.0 %collective-permute-start.1 = (f32[64,384]{1,0:T(8,128)}, f32[64,384]{1,0:T(8,128)S(1)}, u32[]{:S(2)}, u32[]{:S(2)}) collective-permute-start(f32[64,384]{1,0:T(8,128)} %bitcast.8), channel_id=1, source_target_pairs={{0,64},{32,96},{64,128},{96,160},{128,192},{160,224},{192,0},{224,... | collective-permute-start | bytes 294920 | tf_op jit(solution)/shard_map/ppermute | solution.py:295
  6.2 17.8 %collective-permute-start.2 = (f32[64,384]{1,0:T(8,128)}, f32[64,384]{1,0:T(8,128)S(1)}, u32[]{:S(2)}, u32[]{:S(2)}) collective-permute-start(f32[64,384]{1,0:T(8,128)} %bitcast.9), channel_id=1, source_target_pairs={{0,96},{32,128},{64,160},{96,192},{128,224},{160,0},{192,32},{224,... | collective-permute-start | bytes 294920 | tf_op jit(solution)/shard_map/ppermute | solution.py:295
  9.9 14.0 %collective-permute-start.3 = (f32[64,384]{1,0:T(8,128)}, f32[64,384]{1,0:T(8,128)S(1)}, u32[]{:S(2)}, u32[]{:S(2)}) collective-permute-start(f32[64,384]{1,0:T(8,128)} %bitcast.10), channel_id=1, source_target_pairs={{0,128},{32,160},{64,192},{96,224},{128,0},{160,32},{192,64},{224,... | collective-permute-start | bytes 294920 | tf_op jit(solution)/shard_map/ppermute | solution.py:295
  10.4 13.6 %collective-permute-start.4 = (f32[64,384]{1,0:T(8,128)}, f32[64,384]{1,0:T(8,128)S(1)}, u32[]{:S(2)}, u32[]{:S(2)}) collective-permute-start(f32[64,384]{1,0:T(8,128)} %bitcast.11), channel_id=1, source_target_pairs={{0,160},{32,192},{64,224},{96,0},{128,32},{160,64},{192,96},{224,1... | collective-permute-start | bytes 294920 | tf_op jit(solution)/shard_map/ppermute | solution.py:295
  16.1 1.9 copy-start
  18.0 2.7 %copy-start.13 = (f32[384,64]{0,1:T(8,128)S(1)}, f32[384,64]{0,1:T(8,128)}, u32[]{:S(2)}) copy-start(f32[384,64]{0,1:T(8,128)} %param.5) | copy-start | bytes 294916
  19.5 1.2 copy-start.3
  20.7 14.4 %copy-start.5 = (bf16[512,1536]{1,0:T(8,128)(2,1)}, bf16[512,1536]{1,0:T(8,128)(2,1)S(1)}, u32[]{:S(2)}) copy-start(bf16[512,1536]{1,0:T(8,128)(2,1)S(1)} %get-tuple-element.35.turned_low) | copy-start | bytes 4718596
  20.7 9.8 %collective-permute-start.5 = (f32[64,384]{1,0:T(8,128)S(1)}, f32[64,384]{1,0:T(8,128)S(1)}, u32[]{:S(2)}, u32[]{:S(2)}) collective-permute-start(f32[64,384]{1,0:T(8,128)S(1)} %bitcast.12), channel_id=1, source_target_pairs={{0,192},{32,224},{64,0},{96,32},{128,64},{160,96},{192,128},{224,1... | collective-permute-start | bytes 294920 | tf_op jit(solution)/shard_map/ppermute | solution.py:295
  23.1 7.4 %collective-permute-start.6 = (f32[64,384]{1,0:T(8,128)S(1)}, f32[64,384]{1,0:T(8,128)S(1)}, u32[]{:S(2)}, u32[]{:S(2)}) collective-permute-start(f32[64,384]{1,0:T(8,128)S(1)} %bitcast.13), channel_id=1, source_target_pairs={{0,224},{32,0},{64,32},{96,64},{128,96},{160,128},{192,160},{224,1... | collective-permute-start | bytes 294920 | tf_op jit(solution)/shard_map/ppermute | solution.py:295
  24.0 0.6 copy-start.14
  30.5 0.9 copy-start.15
  35.1 2.9 %collective-permute-start.7 = (f32[16,128]{1,0:T(8,128)S(1)}, f32[16,128]{1,0:T(8,128)S(1)}, u32[]{:S(2)}, u32[]{:S(2)}) collective-permute-start(f32[16,128]{1,0:T(8,128)S(1)} %get-tuple-element.27), channel_id=1, source_target_pairs={{0,1},{1,0},{2,3},{3,2},{4,5},{5,4},{6,7},{7,6},{8,9},{9,8},{10,11... | collective-permute-start | bytes 24584 | tf_op jit(solution)/shard_map/ppermute | solution.py:275
  64.7 4.1 %collective-permute-start.8 = (f32[16,128]{1,0:T(8,128)S(1)}, f32[16,128]{1,0:T(8,128)S(1)}, u32[]{:S(2)}, u32[]{:S(2)}) collective-permute-start(f32[16,128]{1,0:T(8,128)S(1)} %shard_map.78), channel_id=1, source_target_pairs={{0,1},{1,0},{2,3},{3,2},{4,5},{5,4},{6,7},{7,6},{8,9},{9,8},{10,11... | collective-permute-start | bytes 24584 | tf_op jit(solution)/shard_map/ppermute | solution.py:275
  91.2 3.8 %collective-permute-start.9 = (f32[16,128]{1,0:T(8,128)S(1)}, f32[16,128]{1,0:T(8,128)S(1)}, u32[]{:S(2)}, u32[]{:S(2)}) collective-permute-start(f32[16,128]{1,0:T(8,128)S(1)} %shard_map.80), channel_id=1, source_target_pairs={{0,1},{1,0},{2,3},{3,2},{4,5},{5,4},{6,7},{7,6},{8,9},{9,8},{10,11... | collective-permute-start | bytes 24584 | tf_op jit(solution)/shard_map/ppermute | solution.py:275
  106.9 0.9 copy-start.11
  107.8 12.1 %all-to-all-start.5 = ((f32[8,8,128]{2,1,0:T(8,128)}), f32[8,8,128]{2,1,0:T(8,128)S(1)}, u32[]{:S(2)}, u32[]{:S(2)}) async-start(f32[8,8,128]{2,1,0:T(8,128)} %get-tuple-element.32.own), calls=%async_computation.5 | async-start | bytes 65536 | tf_op jit(solution)/shard_map/all_to_all | solution.py:286
  111.1 1.4 copy-start.4
  112.5 1.4 copy-start.6
  114.0 1.1 copy-start.12
  123.6 1.0 copy-start.7
  124.6 1.0 copy-start.9
  125.6 8.6 %copy-start.8 = (bf16[1536,384]{1,0:T(8,128)(2,1)S(1)}, bf16[1536,384]{1,0:T(8,128)(2,1)}, u32[]{:S(2)}) copy-start(bf16[1536,384]{1,0:T(8,128)(2,1)} %copy-done.7) | copy-start | bytes 3538948
  125.6 11.9 %collective-permute-start.10 = (f32[16,216,128]{2,1,0:T(8,128)}, f32[16,216,128]{2,1,0:T(8,128)}, u32[]{:S(2)}, u32[]{:S(2)}) collective-permute-start(f32[16,216,128]{2,1,0:T(8,128)} %get-tuple-element.42), channel_id=1, source_target_pairs={{0,1},{1,0},{2,3},{3,2},{4,5},{5,4},{6,7},{7,6},{8,9},{9,8},{10,11... | collective-permute-start | bytes 5308424 | tf_op jit(solution)/shard_map/ppermute | solution.py:343
  127.4 30.5 %all-to-all-start.7 = ((f32[8,192,128]{2,1,0:T(8,128)}), f32[8,192,128]{2,1,0:T(8,128)S(1)}, u32[]{:S(2)}, u32[]{:S(2)}) async-start(f32[8,192,128]{2,1,0:T(8,128)} %shard_map.82), calls=%async_computation.7 | async-start | bytes 1572864 | tf_op jit(solution)/shard_map/all_to_all | solution.py:286
  134.2 1.3 copy-start.10
  157.9 0.9 copy-start.1
  158.8 29.4 %all-to-all-start.6 = ((f32[16,216,128]{2,1,0:T(8,128)}), f32[16,216,128]{2,1,0:T(8,128)S(1)}, u32[]{:S(2)}, u32[]{:S(2)}) async-start(f32[16,216,128]{2,1,0:T(8,128)} %shard_map.85), calls=%async_computation.6 | async-start | bytes 3538944 | tf_op jit(solution)/shard_map/all_to_all | solution.py:348
  163.7 1.1 copy-start.2

commit v2 on v1

--- a/solution.py
+++ b/solution.py
@@ -25,18 +25,19 @@
 
 SMEM = pl.BlockSpec(memory_space=pltpu.SMEM)
 VMEM = pl.BlockSpec(memory_space=pltpu.VMEM)
+HBM = pl.BlockSpec(memory_space=pltpu.HBM)
 
 
 def shaped(shape, dtype=F32):
     return jax.ShapeDtypeStruct(shape, dtype)
 
 
-def call(body, outs, ins, scratch=(), limit=16):
+def call(body, outs, ins, scratch=(), limit=16, places=None):
     return pl.pallas_call(
         body,
         out_shape=outs,
         in_specs=ins,
-        out_specs=jax.tree.map(lambda _: VMEM, outs),
+        out_specs=places or jax.tree.map(lambda _: VMEM, outs),
         scratch_shapes=scratch,
         cost_estimate=pl.CostEstimate(flops=1000000, transcendentals=0, bytes_accessed=4000000),
         compiler_params=pltpu.CompilerParams(vmem_limit_bytes=limit << 20),
@@ -70,7 +71,9 @@
     return jnp.sum(jnp.where(eye, jnp.broadcast_to(row, (BLOCK, BLOCK)), 0.0), axis=1, keepdims=True)
 
 
-def prepare_body(points, high, low, turned_high, turned_low, squares):
+def prepare_body(
+    place, core, nblk, dblk, points, high, low, turned_high, turned_low, squares, th, tl, sems
+):
     for k in range(0, ROWS, 256):
         part = points[k : k + 256, :]
         squares[k : k + 256, :] = jnp.sum(part * part, axis=1, keepdims=True)
@@ -78,8 +81,16 @@
         high[k : k + 256, :] = a
         low[k : k + 256, :] = b
         a, b = halves(part.T)
-        turned_high[:, k : k + 256] = a
-        turned_low[:, k : k + 256] = b
+        th[:, k : k + 256] = a
+        tl[:, k : k + 256] = b
+    copies = [
+        pltpu.make_async_copy(th, turned_high, sems.at[0]),
+        pltpu.make_async_copy(tl, turned_low, sems.at[1]),
+    ]
+    for copy in copies:
+        copy.start()
+    for copy in copies:
+        copy.wait()
 
 
 def row_lse(cost, bias, k):
@@ -88,19 +99,19 @@
     return top + jnp.log(jnp.sum(jnp.exp(scores - top), axis=1, keepdims=True))
 
 
-def live_columns(info):
-    return lax.broadcasted_iota(jnp.int32, (1, COLS), 1) < info[3] * BLOCK
+def live_columns(dblk):
+    return lax.broadcasted_iota(jnp.int32, (1, COLS), 1) < dblk[0] * BLOCK
 
 
 def store_count(out, row, count):
     out[row : row + 1, :] = jnp.full((1, BLOCK), (count * BLOCK).astype(F32))
 
 
-def cost_body(info, high, low, squares, *refs):
+def cost_body(place, core, nblk, dblk, high, low, squares, *refs):
     pieces, (cost, out, turned, data_high, data_low) = refs[:NZ], refs[NZ:]
     square = jnp.zeros((1, COLS), F32)
     for s in range(NZ):
-        z = lax.rem(info[0] + (NZ - s), NZ)
+        z = lax.rem(place[0] + (NZ - s), NZ)
         piece = pieces[s][...]
         square += jnp.sum(piece * piece, axis=0, keepdims=True)
         a, b = halves(piece)
@@ -112,7 +123,7 @@
             turned[q % 2, 0, pl.ds(to, OWN), :] = a[q * OWN : (q + 1) * OWN]
             turned[q % 2, 1, pl.ds(to, OWN), :] = b[q * OWN : (q + 1) * OWN]
     eye = diagonal()
-    bias = jnp.where(live_columns(info), 0.0, -jnp.inf)
+    bias = jnp.where(live_columns(dblk), 0.0, -jnp.inf)
     both = (data_high[...], data_low[...])
     for k in range(0, ROWS, 256):
         cross = dot3((high[k : k + 256, :], low[k : k + 256, :]), both, ((1,), (0,)))
@@ -120,7 +131,7 @@
     out[...] = jnp.zeros((LROWS, BLOCK), F32)
     for k in range(RB):
         out[k : k + 1, :] = to_row(row_lse(cost, bias, k), eye)
-    store_count(out, RB, info[3])
+    store_count(out, RB, dblk[0])
 
 
 def joined(values):
@@ -128,24 +139,24 @@
     return top + jnp.log(jnp.sum(jnp.exp(values - top[None]), axis=0))
 
 
-def column_bias(got, info):
+def column_bias(got, dblk):
     values = got[...]
     total = jnp.sum(values[:, CB, :], axis=0, keepdims=True)
     level = joined(values)
     parts = [-(level[k : k + 1, :] - jnp.log(total)) for k in range(CB)]
-    return jnp.where(live_columns(info), jnp.concatenate(parts, axis=1), -jnp.inf)
-
-
-def row_body(info, got, cost, out):
-    bias = column_bias(got, info)
+    return jnp.where(live_columns(dblk), jnp.concatenate(parts, axis=1), -jnp.inf)
+
+
+def row_body(dblk, got, cost, out):
+    bias = column_bias(got, dblk)
     eye = diagonal()
     out[...] = jnp.zeros((LROWS, BLOCK), F32)
     for k in range(RB):
         out[k : k + 1, :] = to_row(row_lse(cost, bias, k), eye)
-    store_count(out, RB, info[3])
-
-
-def column_body(info, got, cost, out, dual, column):
+    store_count(out, RB, dblk[0])
+
+
+def column_body(nblk, got, cost, out, dual, column):
     values = got[...]
     total = jnp.sum(values[:, RB, :], axis=0, keepdims=True)
     duals = -(joined(values) - jnp.log(total))
@@ -153,7 +164,7 @@
     eye = diagonal()
     tops = []
     for k in range(RB):
-        row = jnp.where(k < info[2], duals[k : k + 1, :], -jnp.inf)
+        row = jnp.where(k < nblk[0], duals[k : k + 1, :], -jnp.inf)
         bias = to_column(row, eye)
         column[k * BLOCK : (k + 1) * BLOCK, :] = bias
         scores = bias - cost[k * BLOCK : (k + 1) * BLOCK, :]
@@ -170,7 +181,7 @@
     level = top + jnp.log(jnp.sum(mass, axis=0, keepdims=True))
     value = jnp.concatenate(
         [level[:, k * BLOCK : (k + 1) * BLOCK] for k in range(CB)]
-        + [jnp.full((1, BLOCK), (info[2] * BLOCK).astype(F32))]
+        + [jnp.full((1, BLOCK), (nblk[0] * BLOCK).astype(F32))]
         + [jnp.zeros((8 - CB - 1, BLOCK), F32)],
         axis=0,
     )
@@ -178,21 +189,40 @@
         out[z] = value
 
 
-def project_noise_body(own, column, cost, turned_high, turned_low, out, weights_high, weights_low):
+def project_noise_body(place, nblk, own, dual, cost, turned_high, turned_low, *refs):
+    outs, (whole, th, tl, weights_high, weights_low, sems) = refs[:NZ], refs[NZ:]
+    copies = [
+        pltpu.make_async_copy(turned_high, th, sems.at[0]),
+        pltpu.make_async_copy(turned_low, tl, sems.at[1]),
+    ]
+    for copy in copies:
+        copy.start()
     level = jnp.concatenate([own[0, k : k + 1, :] for k in range(CB)], axis=1)
-    for k in range(0, ROWS, 256):
-        part = slice(k, k + 256)
-        a, b = halves(jnp.exp(column[part, :] - cost[part, :] - level))
+    eye = diagonal()
+    for k in range(RB):
+        part = slice(k * BLOCK, (k + 1) * BLOCK)
+        row = jnp.where(k < nblk[0], dual[k : k + 1, :], -jnp.inf)
+        a, b = halves(jnp.exp(to_column(row, eye) - cost[part, :] - level))
         weights_high[part, :] = a
         weights_low[part, :] = b
+    for copy in copies:
+        copy.wait()
     both = (weights_high[...], weights_low[...])
     for k in range(0, DIM, 256):
-        some = dot3((turned_high[k : k + 256, :], turned_low[k : k + 256, :]), both, ((1,), (0,)))
+        some = dot3((th[k : k + 256, :], tl[k : k + 256, :]), both, ((1,), (0,)))
         for q in range(256 // CHUNK):
             for c in range(CB):
-                out[k // CHUNK + q, c * CHUNK : (c + 1) * CHUNK, :] = some[
+                whole[k // CHUNK + q, c * CHUNK : (c + 1) * CHUNK, :] = some[
                     q * CHUNK : (q + 1) * CHUNK, c * BLOCK : (c + 1) * BLOCK
                 ]
+    moves = [
+        pltpu.make_async_copy(whole.at[lax.rem(place[0] + s, NZ)], outs[s], sems.at[2 + s])
+        for s in range(NZ)
+    ]
+    for move in moves:
+        move.start()
+    for move in moves:
+        move.wait()
 
 
 def spread(out, some, k):
@@ -203,8 +233,8 @@
             ]
 
 
-def project_data_body(info, got, cost, turned, out, high, low, dual, tops):
-    bias = column_bias(got, info)
+def project_data_body(core, dblk, got, cost, turned, out, high, low, dual, tops):
+    bias = column_bias(got, dblk)
     dual[...] = bias
     eye = diagonal()
     for k in range(RB):
@@ -218,7 +248,7 @@
         a, b = halves(weights)
         high[part, :] = a
         low[part, :] = b
-    other = 1 - info[1]
+    other = 1 - core[0]
     for k in range(ROWS // 256):
         part = slice(k * 256, (k + 1) * 256)
         some = dot3((turned[other, 0], turned[other, 1]), (high[part, :], low[part, :]), ((1,), (1,)))
@@ -227,8 +257,8 @@
         out[p, TOPS:PIECE, :] = tops[...]
 
 
-def project_own_body(info, turned, high, low, out):
-    mine = info[1]
+def project_own_body(core, turned, high, low, out):
+    mine = core[0]
     for k in range(ROWS // 256):
         part = slice(k * 256, (k + 1) * 256)
         some = dot3((turned[mine, 0], turned[mine, 1]), (high[part, :], low[part, :]), ((1,), (1,)))
@@ -250,22 +280,25 @@
         out[p, TOPS:LEVELS, :] = level
 
 
-def finish_noise_body(info, came, out):
+def finish_noise_body(nblk, came, out):
     levels = came[:, LEVELS:PIECE, :]
     shares = jnp.exp(levels - joined(levels)[None])
     for k in range(RB):
         part = slice(k * OWN, (k + 1) * OWN)
         total = jnp.sum(came[:, part, :] * shares[:, k : k + 1, :], axis=0)
-        out[:, k * BLOCK : (k + 1) * BLOCK] = jnp.where(k < info[2], total, 0.0)
-
-
-def finish_data_body(info, came, got, out):
-    levels = got[...]
-    shares = jnp.exp(levels - joined(levels)[None])
+        out[:, k * BLOCK : (k + 1) * BLOCK] = jnp.where(k < nblk[0], total, 0.0)
+
+
+def finish_data_body(place, dblk, got, *refs):
+    came, out = refs[:NZ], refs[NZ]
+    level = joined(got[...])
+    shares = [jnp.exp(got[lax.rem(place[0] + (NZ - s), NZ)] - level) for s in range(NZ)]
     for k in range(CB):
         part = slice(k * CHUNK, (k + 1) * CHUNK)
-        total = jnp.sum(came[:, part, :] * shares[:, k : k + 1, :], axis=0)
-        out[:, k * BLOCK : (k + 1) * BLOCK] = jnp.where(k < info[3], total, 0.0)
+        total = came[0][part, :] * shares[0][k : k + 1, :]
+        for s in range(1, NZ):
+            total += came[s][part, :] * shares[s][k : k + 1, :]
+        out[:, k * BLOCK : (k + 1) * BLOCK] = jnp.where(k < dblk[0], total, 0.0)
 
 
 CORES = [(0, 1), (1, 0)]
@@ -287,10 +320,9 @@
 
 
 def on_device(noise_points, data_points, noise_blocks, data_blocks):
-    info = jnp.concatenate(
-        [lax.axis_index("z").reshape(1), lax.axis_index("c").reshape(1), noise_blocks, data_blocks]
-    )
-    mine = data_points.T
+    place = lax.axis_index("z").reshape(1)
+    core = lax.axis_index("c").reshape(1)
+    mine, place, core = lax.optimization_barrier((data_points.T, place, core))
     pieces = [mine] + [
         lax.ppermute(mine, "z", [(i, (i + s) % NZ) for i in range(NZ)]) for s in range(1, NZ)
     ]
@@ -299,36 +331,64 @@
         (
             shaped((ROWS, DIM), BF16),
             shaped((ROWS, DIM), BF16),
-            shaped((DIM, ROWS), BF16),
-            shaped((DIM, ROWS), BF16),
+            pltpu.HBM((DIM, ROWS), BF16),
+            pltpu.HBM((DIM, ROWS), BF16),
             shaped((ROWS, 1)),
         ),
-        [VMEM],
-    )(noise_points)
+        [SMEM] * 4 + [VMEM],
+        [
+            pltpu.VMEM((DIM, ROWS), BF16),
+            pltpu.VMEM((DIM, ROWS), BF16),
+            pltpu.SemaphoreType.DMA((2,)),
+        ],
+        limit=8,
+        places=(VMEM, VMEM, HBM, HBM, VMEM),
+    )(place, core, noise_blocks, data_blocks, noise_points)
     cost, lse, turned = call(
         cost_body,
         (shaped((ROWS, COLS)), shaped((LROWS, BLOCK)), shaped((NC, 2, DIM // NC, COLS), BF16)),
-        [SMEM] + [VMEM] * (3 + NZ),
+        [SMEM] * 4 + [VMEM] * (3 + NZ),
         [pltpu.VMEM((DIM, COLS), BF16), pltpu.VMEM((DIM, COLS), BF16)],
-    )(info, high, low, squares, *pieces)
+        limit=6,
+    )(place, core, noise_blocks, data_blocks, high, low, squares, *pieces)
     for turn in range(ITERS):
         if turn:
-            lse = call(row_body, shaped((LROWS, BLOCK)), [SMEM, VMEM, VMEM])(info, got, cost)
+            lse = call(row_body, shaped((LROWS, BLOCK)), [SMEM, VMEM, VMEM])(data_blocks, got, cost)
         rows = over_dp(lse)
-        sent, dual, column = call(
+        sent, dual = call(
             column_body,
-            (shaped((NZ, 8, BLOCK)), shaped((LROWS, BLOCK)), shaped((ROWS, 1))),
+            (shaped((NZ, 8, BLOCK)), shaped((LROWS, BLOCK))),
             [SMEM, VMEM, VMEM],
-        )(info, rows, cost)
+            [pltpu.VMEM((ROWS, 1), F32)],
+        )(noise_blocks, rows, cost)
         got = over_noise(sent)
     halfway = call(
         project_noise_body,
-        shaped((NZ, CB * CHUNK, BLOCK)),
-        [VMEM] * 5,
-        [pltpu.VMEM((ROWS, COLS), BF16), pltpu.VMEM((ROWS, COLS), BF16)],
-    )(sent, column, cost, turned_high, turned_low)
+        [pltpu.HBM((CB * CHUNK, BLOCK), F32) for _ in range(NZ)],
+        [SMEM, SMEM, VMEM, VMEM, VMEM, HBM, HBM],
+        [
+            pltpu.VMEM((NZ, CB * CHUNK, BLOCK), F32),
+            pltpu.VMEM((DIM, ROWS), BF16),
+            pltpu.VMEM((DIM, ROWS), BF16),
+            pltpu.VMEM((ROWS, COLS), BF16),
+            pltpu.VMEM((ROWS, COLS), BF16),
+            pltpu.SemaphoreType.DMA((2 + NZ,)),
+        ],
+        places=[HBM] * NZ,
+    )(
+        place,
+        noise_blocks,
+        sent,
+        dual,
+        cost,
+        pltpu.with_memory_space_constraint(turned_high, pltpu.HBM),
+        pltpu.with_memory_space_constraint(turned_low, pltpu.HBM),
+    )
     got, halfway = lax.optimization_barrier((got, halfway))
-    data_came = over_noise(halfway)
+    data_came = [halfway[0]] + [
+        lax.ppermute(halfway[s], "z", [(i, (i + s) % NZ) for i in range(NZ)])
+        for s in range(1, NZ)
+    ]
     theirs, weights_high, weights_low, data_dual, level = call(
         project_data_body,
         (
@@ -338,18 +398,20 @@
             shaped((1, COLS)),
             shaped((2 * RB, BLOCK)),
         ),
-        [SMEM, VMEM, VMEM, VMEM],
-    )(info, got, cost, turned)
+        [SMEM, SMEM, VMEM, VMEM, VMEM],
+    )(core, data_blocks, got, cost, turned)
     came = lax.ppermute(theirs, "c", CORES)
     own = call(
         project_own_body, shaped((NXY, RB * OWN, BLOCK)), [SMEM, VMEM, VMEM, VMEM]
-    )(info, turned, weights_high, weights_low)
+    )(core, turned, weights_high, weights_low)
     merged = call(merge_body, shaped((NXY, PIECE, BLOCK)), [VMEM] * 3)(own, level, came)
     noise_came = lax.all_to_all(merged, ("x", "y"), 0, 0, tiled=True)
-    noise_target = call(finish_noise_body, shaped((OWN, ROWS)), [SMEM, VMEM])(info, noise_came)
+    noise_target = call(finish_noise_body, shaped((OWN, ROWS)), [SMEM, VMEM])(
+        noise_blocks, noise_came
+    )
     data_target = call(
-        finish_data_body, shaped((CHUNK, COLS)), [SMEM, VMEM, VMEM]
-    )(info, data_came, got)
+        finish_data_body, shaped((CHUNK, COLS)), [SMEM, SMEM] + [VMEM] * (1 + NZ)
+    )(place, data_blocks, got, *data_came)
     row_live = jnp.arange(ROWS, dtype=jnp.int32) < noise_blocks[0] * BLOCK
     column_live = jnp.arange(COLS, dtype=jnp.int32) < data_blocks[0] * BLOCK
     noise_potential = jnp.where(row_live, SMOOTHING_TEMP * dual[:RB].reshape(ROWS), 0.0)

time: 190 us -> 155 us (0.82)
  waiting for transfers between devices: 47.8 us -> 23 us
  local copies, waits for them, and re-layouts: 14.8 us -> 1.96 us
  starting transfers between devices: 41.4 us -> 48.6 us
  Pallas kernels: 29.8 us -> 24.1 us
    all_to_all x1, waiting for transfers between devices: 22 us -> 0.01 us  [on_device(): noise_came = lax.all_to_all(merged, ('x', 'y'), 0, 0, tiled=True)]
    all_to_all x2 -> x1, waiting for transfers between devices: 17.4 us -> 0.24 us  [over_noise(): return lax.all_to_all(pieces, 'z', 0, 0, tiled=True)]
    ppermute x0 -> x7, starting transfers between devices: none -> 13.8 us  [on_device(): lax.ppermute(halfway[s], 'z', [(i, (i + s) % NZ) for i in range(NZ)])]
    unnamed x32 -> x20, local copies, waits for them, and re-layouts: 14.7 us -> 1.92 us
    ppermute x0 -> x7, waiting for transfers between devices: none -> 11.9 us  [on_device(): lax.ppermute(halfway[s], 'z', [(i, (i + s) % NZ) for i in range(NZ)])]
    all_to_all x2 -> x1, starting transfers between devices: 10.2 us -> 3.33 us  [over_noise(): return lax.all_to_all(pieces, 'z', 0, 0, tiled=True)]
    pallas_call x8, Pallas kernels: 16 us -> 13.1 us  [the longest x1 6.55 us: on_device(): call(project_noise_body, [pltpu.HBM((CB * CHUNK, BLOCK), F32) for _ in ra...]
    ppermute x1, waiting for transfers between devices: 0.01 us -> 1.91 us  [on_device(): came = lax.ppermute(theirs, 'c', CORES)]
  transfers between devices with their start and end apart: 14 -> 20, of which waited for: 6 -> 12; matrix products, arithmetic and copies ran while one was open for 1% -> 1% of each run, Pallas kernels for 7% -> 8%
where the time goes in v2:
time: 155 us; the launch traced here: 154 us
  blocking collectives  53.2 us (34%)
  starting transfers between devices  48.6 us (31%)
  Pallas kernels  24.1 us (16%)
  waiting for transfers between devices  23 us (15%)
  between operations  2.15 us (1%)
  local copies, waits for them, and re-layouts  1.96 us (1%)
    all_to_all x3, blocking collectives, over_dp(): lax.all_to_all(jnp.broadcast_to(both[None], (NXY, LROWS, BLOCK)), ('x', '...  32.9 us
    all_to_all x2, blocking collectives, over_noise(): return lax.all_to_all(pieces, 'z', 0, 0, tiled=True)  20.3 us
    ppermute x7, starting transfers between devices, on_device(): lax.ppermute(mine, 'z', [(i, (i + s) % NZ) for i in range(NZ)])  17.3 us
    ppermute x7, starting transfers between devices, on_device(): lax.ppermute(halfway[s], 'z', [(i, (i + s) % NZ) for i in range(NZ)])  13.8 us
    ppermute x7, waiting for transfers between devices, on_device(): lax.ppermute(halfway[s], 'z', [(i, (i + s) % NZ) for i in range(NZ)])  11.9 us
    ppermute x3, starting transfers between devices, over_dp(): came = lax.ppermute(lse, 'c', CORES)  7.07 us
    pallas_call x1, Pallas kernels, on_device(): call(project_noise_body, [pltpu.HBM((CB * CHUNK, BLOCK), F32) for _ in ra...  6.55 us
    ppermute x7, waiting for transfers between devices, on_device(): lax.ppermute(mine, 'z', [(i, (i + s) % NZ) for i in range(NZ)])  6.46 us
  transfers between devices with their start and end apart: 20, of which 12 were waited for; matrix products, arithmetic and copies ran while one was open for 1% of the time, Pallas kernels for 8%

profile of v2, /device:TPU:1, one launch (start us, length us, event | category | flops | bytes accessed | tf_op | source)
XLA Modules:
  0.0 154.4 jit_solution(8094468023965883836)
XLA Ops:
  0.6 2.5 %collective-permute-start = (f32[64,384]{1,0:T(8,128)}, f32[64,384]{1,0:T(8,128)S(1)}, u32[]{:S(2)}, u32[]{:S(2)}) collective-permute-start(f32[64,384]{1,0:T(8,128)} %bitcast.7), channel_id=1, source_target_pairs={{0,32},{32,64},{64,96},{96,128},{128,160},{160,192},{192,224},{224... | collective-permute-start | bytes 294920 | tf_op jit(solution)/shard_map/ppermute | solution.py:327
  3.2 3.0 %collective-permute-start.1 = (f32[64,384]{1,0:T(8,128)}, f32[64,384]{1,0:T(8,128)S(1)}, u32[]{:S(2)}, u32[]{:S(2)}) collective-permute-start(f32[64,384]{1,0:T(8,128)} %bitcast.8), channel_id=1, source_target_pairs={{0,64},{32,96},{64,128},{96,160},{128,192},{160,224},{192,0},{224,... | collective-permute-start | bytes 294920 | tf_op jit(solution)/shard_map/ppermute | solution.py:327
  6.2 3.8 %collective-permute-start.2 = (f32[64,384]{1,0:T(8,128)}, f32[64,384]{1,0:T(8,128)S(1)}, u32[]{:S(2)}, u32[]{:S(2)}) collective-permute-start(f32[64,384]{1,0:T(8,128)} %bitcast.9), channel_id=1, source_target_pairs={{0,96},{32,128},{64,160},{96,192},{128,224},{160,0},{192,32},{224,... | collective-permute-start | bytes 294920 | tf_op jit(solution)/shard_map/ppermute | solution.py:327
  9.9 0.5 collective-permute-start.3
  10.4 4.5 %collective-permute-start.4 = (f32[64,384]{1,0:T(8,128)}, f32[64,384]{1,0:T(8,128)S(1)}, u32[]{:S(2)}, u32[]{:S(2)}) collective-permute-start(f32[64,384]{1,0:T(8,128)} %bitcast.11), channel_id=1, source_target_pairs={{0,160},{32,192},{64,224},{96,0},{128,32},{160,64},{192,96},{224,1... | collective-permute-start | bytes 294920 | tf_op jit(solution)/shard_map/ppermute | solution.py:327
  14.8 0.0 collective-permute-done.refs_1_
  14.9 2.4 %collective-permute-start.5 = (f32[64,384]{1,0:T(8,128)}, f32[64,384]{1,0:T(8,128)S(1)}, u32[]{:S(2)}, u32[]{:S(2)}) collective-permute-start(f32[64,384]{1,0:T(8,128)} %bitcast.12), channel_id=1, source_target_pairs={{0,192},{32,224},{64,0},{96,32},{128,64},{160,96},{192,128},{224,1... | collective-permute-start | bytes 294920 | tf_op jit(solution)/shard_map/ppermute | solution.py:327
  17.2 0.0 collective-permute-done.1.refs_2_
  17.2 0.7 collective-permute-start.6
  19.3 1.9 %copy-done = f32[1536,512]{1,0:T(8,128)S(1)} copy-done((f32[1536,512]{1,0:T(8,128)S(1)}, f32[1536,512]{1,0:T(8,128)}, u32[]{:S(2)}) %copy-start) | copy-done | bytes 3145752
  21.2 3.1 %shard_map.75 = (bf16[1536,512]{1,0:T(8,128)(2,1)S(1)}, bf16[1536,512]{1,0:T(8,128)(2,1)S(1)}, bf16[512,1536]{1,0:T(8,128)(2,1)}, bf16[512,1536]{1,0:T(8,128)(2,1)}, f32[1536,1]{1,0:T(8,128)S(1)}) custom-call(s32[1]{0:T(128)} %bitcast.2.place, s32[1]{0:T(128)} %bitcast.3.core, s32[1]{0:T(128)S(6)} %copy.8.nblk, s32[1]{0:T(128)S(6)} %copy.9.dblk, ...), custom_call_target="tpu_custom_call" | custom-call | flops 1000000 | bytes 4000000 | tf_op jit(solution)/shard_map/pallas_call | solution.py:329
  24.3 0.0 collective-permute-done.2.refs_3_
  24.3 0.0 collective-permute-done.3.refs_4_
  24.3 0.0 collective-permute-done.4.refs_5_
  24.3 5.7 %collective-permute-done.5.refs_6_ = f32[64,384]{1,0:T(8,128)S(1)} collective-permute-done((f32[64,384]{1,0:T(8,128)}, f32[64,384]{1,0:T(8,128)S(1)}, u32[]{:S(2)}, u32[]{:S(2)}) %collective-permute-start.5) | collective-permute-done | bytes 98336 | tf_op jit(solution)/shard_map/ppermute | solution.py:327
  30.0 0.7 collective-permute-done.6.refs_7_
  30.8 3.1 %shard_map.76 = (f32[1536,384]{1,0:T(8,128)S(1)}, f32[16,128]{1,0:T(8,128)S(1)}, bf16[2,2,256,384]{3,2,1,0:T(8,128)(2,1)S(1)}) custom-call(s32[1]{0:T(128)} %bitcast.2.place, s32[1]{0:T(128)} %bitcast.3.core, s32[1]{0:T(128)S(6)} %copy.8.nblk, s32[1]{0:T(128)S(6)} %copy.9.dblk, bf16[1536,512]{1,0:T(8,128)(2,1)S(1)} %get-tuple-element.43.high, ...), custom_call_target="tpu_custom_call" | custom-call | flops 1000000 | bytes 4000000 | tf_op jit(solution)/shard_map/pallas_call | solution.py:347
  33.9 0.8 collective-permute-start.7
  34.7 0.8 collective-permute-done.7
  35.5 0.1 add_select_fusion.2
  35.6 13.2 %all_to_all.35.got = f32[16,16,128]{2,1,0:T(8,128)S(1)} all-to-all(f32[16,16,128]{2,1,0:T(8,128)S(1)} %broadcast_in_dim.12), channel_id=1, replica_groups=mesh['z'=8,'x'=4,'y'=4,'c'=2] {'x','y'}, dimensions={0} | all-to-all | bytes 262144 | tf_op jit(solution)/shard_map/all_to_all | solution.py:313
  48.8 0.8 shard_map.77
  49.6 11.1 %all_to_all.36.got = f32[8,8,128]{2,1,0:T(8,128)S(1)} all-to-all(f32[8,8,128]{2,1,0:T(8,128)S(1)} %get-tuple-element.49), channel_id=1, replica_groups=mesh['z'=8,'x'=4,'y'=4,'c'=2] {'z'}, dimensions={0} | all-to-all | bytes 65536 | tf_op jit(solution)/shard_map/all_to_all | solution.py:319
  60.7 1.0 shard_map.78
  61.7 3.3 %collective-permute-start.8 = (f32[16,128]{1,0:T(8,128)S(1)}, f32[16,128]{1,0:T(8,128)S(1)}, u32[]{:S(2)}, u32[]{:S(2)}) collective-permute-start(f32[16,128]{1,0:T(8,128)S(1)} %shard_map.78), channel_id=1, source_target_pairs={{0,1},{1,0},{2,3},{3,2},{4,5},{5,4},{6,7},{7,6},{8,9},{9,8},{10,11... | collective-permute-start | bytes 24584 | tf_op jit(solution)/shard_map/ppermute | solution.py:308
  65.0 0.8 collective-permute-done.8
  65.8 0.1 add_select_fusion.1
  65.9 9.8 %all_to_all.37.got = f32[16,16,128]{2,1,0:T(8,128)S(1)} all-to-all(f32[16,16,128]{2,1,0:T(8,128)S(1)} %broadcast_in_dim.14), channel_id=1, replica_groups=mesh['z'=8,'x'=4,'y'=4,'c'=2] {'x','y'}, dimensions={0} | all-to-all | bytes 262144 | tf_op jit(solution)/shard_map/all_to_all | solution.py:313
  75.7 0.8 shard_map.79
  76.5 9.2 %all_to_all.38.got = f32[8,8,128]{2,1,0:T(8,128)S(1)} all-to-all(f32[8,8,128]{2,1,0:T(8,128)S(1)} %get-tuple-element.50), channel_id=1, replica_groups=mesh['z'=8,'x'=4,'y'=4,'c'=2] {'z'}, dimensions={0} | all-to-all | bytes 65536 | tf_op jit(solution)/shard_map/all_to_all | solution.py:319
  85.7 1.0 shard_map.80
  86.7 3.0 %collective-permute-start.9 = (f32[16,128]{1,0:T(8,128)S(1)}, f32[16,128]{1,0:T(8,128)S(1)}, u32[]{:S(2)}, u32[]{:S(2)}) collective-permute-start(f32[16,128]{1,0:T(8,128)S(1)} %shard_map.80), channel_id=1, source_target_pairs={{0,1},{1,0},{2,3},{3,2},{4,5},{5,4},{6,7},{7,6},{8,9},{9,8},{10,11... | collective-permute-start | bytes 24584 | tf_op jit(solution)/shard_map/ppermute | solution.py:308
  89.8 0.8 collective-permute-done.9
  90.6 0.1 add_select_fusion
  90.7 9.8 %all_to_all.39.got = f32[16,16,128]{2,1,0:T(8,128)S(1)} all-to-all(f32[16,16,128]{2,1,0:T(8,128)S(1)} %broadcast_in_dim.28), channel_id=1, replica_groups=mesh['z'=8,'x'=4,'y'=4,'c'=2] {'x','y'}, dimensions={0} | all-to-all | bytes 262144 | tf_op jit(solution)/shard_map/all_to_all | solution.py:313
  100.5 1.4 shard_map.81
  101.8 3.3 %all-to-all-start.5 = ((f32[8,8,128]{2,1,0:T(8,128)}), f32[8,8,128]{2,1,0:T(8,128)S(1)}, u32[]{:S(2)}, u32[]{:S(2)}) async-start(f32[8,8,128]{2,1,0:T(8,128)} %get-tuple-element.52.own), calls=%async_computation.5 | async-start | bytes 65536 | tf_op jit(solution)/shard_map/all_to_all | solution.py:319
  105.2 6.6 %shard_map.82 = (f32[192,128]{1,0:T(8,128)}, f32[192,128]{1,0:T(8,128)}, f32[192,128]{1,0:T(8,128)}, f32[192,128]{1,0:T(8,128)}, f32[192,128]{1,0:T(8,128)}, /*i...) custom-call(s32[1]{0:T(128)} %bitcast.2.place, s32[1]{0:T(128)S(6)} %copy.8.nblk, ...), custom_call_target="tpu_custom_call" | custom-call | flops 1000000 | bytes 4000000 | tf_op jit(solution)/shard_map/pallas_call | solution.py:365
  111.7 0.2 all-to-all-done.5.got
  112.0 1.9 %shard_map.83 = (f32[16,216,128]{2,1,0:T(8,128)S(1)}, bf16[1536,384]{1,0:T(8,128)(2,1)S(1)}, bf16[1536,384]{1,0:T(8,128)(2,1)S(1)}, f32[1,384]{1,0:T(1,128)S(1)}, f32[24,128]{1,0:T(8,128)S(1)}) custom-call(s32[1]{0:T(128)} %bitcast.3.core, s32[1]{0:T(128)S(6)} %copy.9.dblk, f32[8,8,128]{2,1,0:T(8,128)S(1)} %all-to-all-done.5.got, ...), custom_call_target="tpu_custom_call" | custom-call | flops 1000000 | bytes 4000000 | tf_op jit(solution)/shard_map/pallas_call | solution.py:392
  113.9 3.0 %collective-permute-start.10 = (f32[16,216,128]{2,1,0:T(8,128)S(1)}, f32[16,216,128]{2,1,0:T(8,128)S(1)}, u32[]{:S(2)}, u32[]{:S(2)}) collective-permute-start(f32[16,216,128]{2,1,0:T(8,128)S(1)} %get-tuple-element.69), channel_id=1, source_target_pairs={{0,1},{1,0},{2,3},{3,2},{4,5},{5,4},{6,7},{7,6},{8,9},{9,8},{10,11... | collective-permute-start | bytes 5308424 | tf_op jit(solution)/shard_map/ppermute | solution.py:403
  116.9 1.4 shard_map.84.own
  118.3 1.9 %collective-permute-done.10.came = f32[16,216,128]{2,1,0:T(8,128)S(1)} collective-permute-done((f32[16,216,128]{2,1,0:T(8,128)S(1)}, f32[16,216,128]{2,1,0:T(8,128)S(1)}, u32[]{:S(2)}, u32[]{:S(2)}) %collective-permute-start.10) | collective-permute-done | bytes 1769504 | tf_op jit(solution)/shard_map/ppermute | solution.py:403
  120.2 1.5 shard_map.85
  121.7 0.0 copy-start.1
  121.7 4.1 %all-to-all-start.6 = ((f32[16,216,128]{2,1,0:T(8,128)}), f32[16,216,128]{2,1,0:T(8,128)S(1)}, u32[]{:S(2)}, u32[]{:S(2)}) async-start(f32[16,216,128]{2,1,0:T(8,128)} %shard_map.85), calls=%async_computation.6 | async-start | bytes 3538944 | tf_op jit(solution)/shard_map/all_to_all | solution.py:408
  125.8 0.6 bitcast_select_fusion
  126.4 0.3 collective-permute-start.11
  126.7 2.1 %collective-permute-start.12 = (f32[192,128]{1,0:T(8,128)S(1)}, f32[192,128]{1,0:T(8,128)S(1)}, u32[]{:S(2)}, u32[]{:S(2)}) collective-permute-start(f32[192,128]{1,0:T(8,128)S(1)} %copy-done.8), channel_id=1, source_target_pairs={{0,64},{32,96},{64,128},{96,160},{128,192},{160,224},{192,0},{224,... | collective-permute-start | bytes 294920 | tf_op jit(solution)/shard_map/ppermute | solution.py:389
  128.8 2.4 %collective-permute-start.13 = (f32[192,128]{1,0:T(8,128)S(1)}, f32[192,128]{1,0:T(8,128)S(1)}, u32[]{:S(2)}, u32[]{:S(2)}) collective-permute-start(f32[192,128]{1,0:T(8,128)S(1)} %copy-done.7), channel_id=1, source_target_pairs={{0,96},{32,128},{64,160},{96,192},{128,224},{160,0},{192,32},{224,... | collective-permute-start | bytes 294920 | tf_op jit(solution)/shard_map/ppermute | solution.py:389
  131.2 2.1 %collective-permute-start.14 = (f32[192,128]{1,0:T(8,128)S(1)}, f32[192,128]{1,0:T(8,128)S(1)}, u32[]{:S(2)}, u32[]{:S(2)}) collective-permute-start(f32[192,128]{1,0:T(8,128)S(1)} %copy-done.6), channel_id=1, source_target_pairs={{0,128},{32,160},{64,192},{96,224},{128,0},{160,32},{192,64},{224,... | collective-permute-start | bytes 294920 | tf_op jit(solution)/shard_map/ppermute | solution.py:389
  133.3 2.4 %collective-permute-start.15 = (f32[192,128]{1,0:T(8,128)S(1)}, f32[192,128]{1,0:T(8,128)S(1)}, u32[]{:S(2)}, u32[]{:S(2)}) collective-permute-start(f32[192,128]{1,0:T(8,128)S(1)} %copy-done.5), channel_id=1, source_target_pairs={{0,160},{32,192},{64,224},{96,0},{128,32},{160,64},{192,96},{224,1... | collective-permute-start | bytes 294920 | tf_op jit(solution)/shard_map/ppermute | solution.py:389
  135.7 0.0 collective-permute-done.11.refs_1_
  135.7 3.4 %collective-permute-start.16 = (f32[192,128]{1,0:T(8,128)S(1)}, f32[192,128]{1,0:T(8,128)S(1)}, u32[]{:S(2)}, u32[]{:S(2)}) collective-permute-start(f32[192,128]{1,0:T(8,128)S(1)} %copy-done.4), channel_id=1, source_target_pairs={{0,192},{32,224},{64,0},{96,32},{128,64},{160,96},{192,128},{224,1... | collective-permute-start | bytes 294920 | tf_op jit(solution)/shard_map/ppermute | solution.py:389
  139.1 0.0 collective-permute-done.12.refs_2_
  139.1 1.2 collective-permute-start.17
  140.3 0.6 fusion.3
  140.9 0.5 collective-permute-done.13.refs_3_
  141.4 2.7 %collective-permute-done.14.refs_4_ = f32[192,128]{1,0:T(8,128)S(1)} collective-permute-done((f32[192,128]{1,0:T(8,128)S(1)}, f32[192,128]{1,0:T(8,128)S(1)}, u32[]{:S(2)}, u32[]{:S(2)}) %collective-permute-start.14) | collective-permute-done | bytes 98336 | tf_op jit(solution)/shard_map/ppermute | solution.py:389
  144.1 1.8 %collective-permute-done.15.refs_5_ = f32[192,128]{1,0:T(8,128)S(1)} collective-permute-done((f32[192,128]{1,0:T(8,128)S(1)}, f32[192,128]{1,0:T(8,128)S(1)}, u32[]{:S(2)}, u32[]{:S(2)}) %collective-permute-start.15) | collective-permute-done | bytes 98336 | tf_op jit(solution)/shard_map/ppermute | solution.py:389
  145.8 6.2 %collective-permute-done.16.refs_6_ = f32[192,128]{1,0:T(8,128)S(1)} collective-permute-done((f32[192,128]{1,0:T(8,128)S(1)}, f32[192,128]{1,0:T(8,128)S(1)}, u32[]{:S(2)}, u32[]{:S(2)}) %collective-permute-start.16) | collective-permute-done | bytes 98336 | tf_op jit(solution)/shard_map/ppermute | solution.py:389
  152.1 0.7 collective-permute-done.17.refs_7_
  152.8 0.7 shard_map.87
  153.5 0.9 shard_map.86
  (24 shorter events, 0.1 us)
Async XLA Ops:
  0.6 14.2 %collective-permute-start = (f32[64,384]{1,0:T(8,128)}, f32[64,384]{1,0:T(8,128)S(1)}, u32[]{:S(2)}, u32[]{:S(2)}) collective-permute-start(f32[64,384]{1,0:T(8,128)} %bitcast.7), channel_id=1, source_target_pairs={{0,32},{32,64},{64,96},{96,128},{128,160},{160,192},{192,224},{224... | collective-permute-start | bytes 294920 | tf_op jit(solution)/shard_map/ppermute | solution.py:327
  3.2 14.1 %collective-permute-start.1 = (f32[64,384]{1,0:T(8,128)}, f32[64,384]{1,0:T(8,128)S(1)}, u32[]{:S(2)}, u32[]{:S(2)}) collective-permute-start(f32[64,384]{1,0:T(8,128)} %bitcast.8), channel_id=1, source_target_pairs={{0,64},{32,96},{64,128},{96,160},{128,192},{160,224},{192,0},{224,... | collective-permute-start | bytes 294920 | tf_op jit(solution)/shard_map/ppermute | solution.py:327
  6.2 18.1 %collective-permute-start.2 = (f32[64,384]{1,0:T(8,128)}, f32[64,384]{1,0:T(8,128)S(1)}, u32[]{:S(2)}, u32[]{:S(2)}) collective-permute-start(f32[64,384]{1,0:T(8,128)} %bitcast.9), channel_id=1, source_target_pairs={{0,96},{32,128},{64,160},{96,192},{128,224},{160,0},{192,32},{224,... | collective-permute-start | bytes 294920 | tf_op jit(solution)/shard_map/ppermute | solution.py:327
  9.9 14.4 %collective-permute-start.3 = (f32[64,384]{1,0:T(8,128)}, f32[64,384]{1,0:T(8,128)S(1)}, u32[]{:S(2)}, u32[]{:S(2)}) collective-permute-start(f32[64,384]{1,0:T(8,128)} %bitcast.10), channel_id=1, source_target_pairs={{0,128},{32,160},{64,192},{96,224},{128,0},{160,32},{192,64},{224,... | collective-permute-start | bytes 294920 | tf_op jit(solution)/shard_map/ppermute | solution.py:327
  10.4 13.9 %collective-permute-start.4 = (f32[64,384]{1,0:T(8,128)}, f32[64,384]{1,0:T(8,128)S(1)}, u32[]{:S(2)}, u32[]{:S(2)}) collective-permute-start(f32[64,384]{1,0:T(8,128)} %bitcast.11), channel_id=1, source_target_pairs={{0,160},{32,192},{64,224},{96,0},{128,32},{160,64},{192,96},{224,1... | collective-permute-start | bytes 294920 | tf_op jit(solution)/shard_map/ppermute | solution.py:327
  14.9 15.2 %collective-permute-start.5 = (f32[64,384]{1,0:T(8,128)}, f32[64,384]{1,0:T(8,128)S(1)}, u32[]{:S(2)}, u32[]{:S(2)}) collective-permute-start(f32[64,384]{1,0:T(8,128)} %bitcast.12), channel_id=1, source_target_pairs={{0,192},{32,224},{64,0},{96,32},{128,64},{160,96},{192,128},{224,1... | collective-permute-start | bytes 294920 | tf_op jit(solution)/shard_map/ppermute | solution.py:327
  17.2 13.5 %collective-permute-start.6 = (f32[64,384]{1,0:T(8,128)}, f32[64,384]{1,0:T(8,128)S(1)}, u32[]{:S(2)}, u32[]{:S(2)}) collective-permute-start(f32[64,384]{1,0:T(8,128)} %bitcast.13), channel_id=1, source_target_pairs={{0,224},{32,0},{64,32},{96,64},{128,96},{160,128},{192,160},{224,1... | collective-permute-start | bytes 294920 | tf_op jit(solution)/shard_map/ppermute | solution.py:327
  19.3 1.9 %copy-start = (f32[1536,512]{1,0:T(8,128)S(1)}, f32[1536,512]{1,0:T(8,128)}, u32[]{:S(2)}) copy-start(f32[1536,512]{1,0:T(8,128)} %points.1) | copy-start | bytes 9437188
  21.2 9.6 %copy-start.2 = (f32[384,64]{0,1:T(8,128)S(1)}, f32[384,64]{0,1:T(8,128)}, u32[]{:S(2)}) copy-start(f32[384,64]{0,1:T(8,128)} %param.5) | copy-start | bytes 294916
  33.9 1.6 %collective-permute-start.7 = (f32[16,128]{1,0:T(8,128)S(1)}, f32[16,128]{1,0:T(8,128)S(1)}, u32[]{:S(2)}, u32[]{:S(2)}) collective-permute-start(f32[16,128]{1,0:T(8,128)S(1)} %get-tuple-element.47), channel_id=1, source_target_pairs={{0,1},{1,0},{2,3},{3,2},{4,5},{5,4},{6,7},{7,6},{8,9},{9,8},{10,11... | collective-permute-start | bytes 24584 | tf_op jit(solution)/shard_map/ppermute | solution.py:308
  61.7 4.1 %collective-permute-start.8 = (f32[16,128]{1,0:T(8,128)S(1)}, f32[16,128]{1,0:T(8,128)S(1)}, u32[]{:S(2)}, u32[]{:S(2)}) collective-permute-start(f32[16,128]{1,0:T(8,128)S(1)} %shard_map.78), channel_id=1, source_target_pairs={{0,1},{1,0},{2,3},{3,2},{4,5},{5,4},{6,7},{7,6},{8,9},{9,8},{10,11... | collective-permute-start | bytes 24584 | tf_op jit(solution)/shard_map/ppermute | solution.py:308
  86.7 3.8 %collective-permute-start.9 = (f32[16,128]{1,0:T(8,128)S(1)}, f32[16,128]{1,0:T(8,128)S(1)}, u32[]{:S(2)}, u32[]{:S(2)}) collective-permute-start(f32[16,128]{1,0:T(8,128)S(1)} %shard_map.80), channel_id=1, source_target_pairs={{0,1},{1,0},{2,3},{3,2},{4,5},{5,4},{6,7},{7,6},{8,9},{9,8},{10,11... | collective-permute-start | bytes 24584 | tf_op jit(solution)/shard_map/ppermute | solution.py:308
  101.8 10.1 %all-to-all-start.5 = ((f32[8,8,128]{2,1,0:T(8,128)}), f32[8,8,128]{2,1,0:T(8,128)S(1)}, u32[]{:S(2)}, u32[]{:S(2)}) async-start(f32[8,8,128]{2,1,0:T(8,128)} %get-tuple-element.52.own), calls=%async_computation.5 | async-start | bytes 65536 | tf_op jit(solution)/shard_map/all_to_all | solution.py:319
  113.9 6.3 %collective-permute-start.10 = (f32[16,216,128]{2,1,0:T(8,128)S(1)}, f32[16,216,128]{2,1,0:T(8,128)S(1)}, u32[]{:S(2)}, u32[]{:S(2)}) collective-permute-start(f32[16,216,128]{2,1,0:T(8,128)S(1)} %get-tuple-element.69), channel_id=1, source_target_pairs={{0,1},{1,0},{2,3},{3,2},{4,5},{5,4},{6,7},{7,6},{8,9},{9,8},{10,11... | collective-permute-start | bytes 5308424 | tf_op jit(solution)/shard_map/ppermute | solution.py:403
  121.7 4.7 %copy-start.9 = (f32[192,128]{1,0:T(8,128)S(1)}, f32[192,128]{1,0:T(8,128)}, u32[]{:S(2)}) copy-start(f32[192,128]{1,0:T(8,128)} %get-tuple-element.71) | copy-start | bytes 294916
  121.7 5.0 %copy-start.8 = (f32[192,128]{1,0:T(8,128)S(1)}, f32[192,128]{1,0:T(8,128)}, u32[]{:S(2)}) copy-start(f32[192,128]{1,0:T(8,128)} %get-tuple-element.72) | copy-start | bytes 294916
  121.7 7.1 %copy-start.7 = (f32[192,128]{1,0:T(8,128)S(1)}, f32[192,128]{1,0:T(8,128)}, u32[]{:S(2)}) copy-start(f32[192,128]{1,0:T(8,128)} %get-tuple-element.73) | copy-start | bytes 294916
  121.7 9.5 %copy-start.6 = (f32[192,128]{1,0:T(8,128)S(1)}, f32[192,128]{1,0:T(8,128)}, u32[]{:S(2)}) copy-start(f32[192,128]{1,0:T(8,128)} %get-tuple-element.74) | copy-start | bytes 294916
  121.7 11.6 %copy-start.5 = (f32[192,128]{1,0:T(8,128)S(1)}, f32[192,128]{1,0:T(8,128)}, u32[]{:S(2)}) copy-start(f32[192,128]{1,0:T(8,128)} %get-tuple-element.75) | copy-start | bytes 294916
  121.7 14.0 %copy-start.4 = (f32[192,128]{1,0:T(8,128)S(1)}, f32[192,128]{1,0:T(8,128)}, u32[]{:S(2)}) copy-start(f32[192,128]{1,0:T(8,128)} %get-tuple-element.76) | copy-start | bytes 294916
  121.7 17.4 %copy-start.3 = (f32[192,128]{1,0:T(8,128)S(1)}, f32[192,128]{1,0:T(8,128)}, u32[]{:S(2)}) copy-start(f32[192,128]{1,0:T(8,128)} %get-tuple-element.77) | copy-start | bytes 294916
  121.7 31.1 %copy-start.1 = (f32[192,128]{1,0:T(8,128)S(1)}, f32[192,128]{1,0:T(8,128)}, u32[]{:S(2)}) copy-start(f32[192,128]{1,0:T(8,128)} %get-tuple-element.70.refs_0_) | copy-start | bytes 294916
  121.7 31.8 %all-to-all-start.6 = ((f32[16,216,128]{2,1,0:T(8,128)}), f32[16,216,128]{2,1,0:T(8,128)S(1)}, u32[]{:S(2)}, u32[]{:S(2)}) async-start(f32[16,216,128]{2,1,0:T(8,128)} %shard_map.85), calls=%async_computation.6 | async-start | bytes 3538944 | tf_op jit(solution)/shard_map/all_to_all | solution.py:408
  126.4 9.3 %collective-permute-start.11 = (f32[192,128]{1,0:T(8,128)S(1)}, f32[192,128]{1,0:T(8,128)S(1)}, u32[]{:S(2)}, u32[]{:S(2)}) collective-permute-start(f32[192,128]{1,0:T(8,128)S(1)} %copy-done.9), channel_id=1, source_target_pairs={{0,32},{32,64},{64,96},{96,128},{128,160},{160,192},{192,224},{224... | collective-permute-start | bytes 294920 | tf_op jit(solution)/shard_map/ppermute | solution.py:389
  126.7 12.4 %collective-permute-start.12 = (f32[192,128]{1,0:T(8,128)S(1)}, f32[192,128]{1,0:T(8,128)S(1)}, u32[]{:S(2)}, u32[]{:S(2)}) collective-permute-start(f32[192,128]{1,0:T(8,128)S(1)} %copy-done.8), channel_id=1, source_target_pairs={{0,64},{32,96},{64,128},{96,160},{128,192},{160,224},{192,0},{224,... | collective-permute-start | bytes 294920 | tf_op jit(solution)/shard_map/ppermute | solution.py:389
  128.8 12.6 %collective-permute-start.13 = (f32[192,128]{1,0:T(8,128)S(1)}, f32[192,128]{1,0:T(8,128)S(1)}, u32[]{:S(2)}, u32[]{:S(2)}) collective-permute-start(f32[192,128]{1,0:T(8,128)S(1)} %copy-done.7), channel_id=1, source_target_pairs={{0,96},{32,128},{64,160},{96,192},{128,224},{160,0},{192,32},{224,... | collective-permute-start | bytes 294920 | tf_op jit(solution)/shard_map/ppermute | solution.py:389
  131.2 12.8 %collective-permute-start.14 = (f32[192,128]{1,0:T(8,128)S(1)}, f32[192,128]{1,0:T(8,128)S(1)}, u32[]{:S(2)}, u32[]{:S(2)}) collective-permute-start(f32[192,128]{1,0:T(8,128)S(1)} %copy-done.6), channel_id=1, source_target_pairs={{0,128},{32,160},{64,192},{96,224},{128,0},{160,32},{192,64},{224,... | collective-permute-start | bytes 294920 | tf_op jit(solution)/shard_map/ppermute | solution.py:389
  133.3 12.6 %collective-permute-start.15 = (f32[192,128]{1,0:T(8,128)S(1)}, f32[192,128]{1,0:T(8,128)S(1)}, u32[]{:S(2)}, u32[]{:S(2)}) collective-permute-start(f32[192,128]{1,0:T(8,128)S(1)} %copy-done.5), channel_id=1, source_target_pairs={{0,160},{32,192},{64,224},{96,0},{128,32},{160,64},{192,96},{224,1... | collective-permute-start | bytes 294920 | tf_op jit(solution)/shard_map/ppermute | solution.py:389
  135.7 16.3 %collective-permute-start.16 = (f32[192,128]{1,0:T(8,128)S(1)}, f32[192,128]{1,0:T(8,128)S(1)}, u32[]{:S(2)}, u32[]{:S(2)}) collective-permute-start(f32[192,128]{1,0:T(8,128)S(1)} %copy-done.4), channel_id=1, source_target_pairs={{0,192},{32,224},{64,0},{96,32},{128,64},{160,96},{192,128},{224,1... | collective-permute-start | bytes 294920 | tf_op jit(solution)/shard_map/ppermute | solution.py:389
  139.1 13.7 %collective-permute-start.17 = (f32[192,128]{1,0:T(8,128)S(1)}, f32[192,128]{1,0:T(8,128)S(1)}, u32[]{:S(2)}, u32[]{:S(2)}) collective-permute-start(f32[192,128]{1,0:T(8,128)S(1)} %copy-done.3), channel_id=1, source_target_pairs={{0,224},{32,0},{64,32},{96,64},{128,96},{160,128},{192,160},{224,1... | collective-permute-start | bytes 294920 | tf_op jit(solution)/shard_map/ppermute | solution.py:389

commit v3 on v2

--- a/solution.py
+++ b/solution.py
@@ -78,8 +78,11 @@
         part = points[k : k + 256, :]
         squares[k : k + 256, :] = jnp.sum(part * part, axis=1, keepdims=True)
         a, b = halves(part)
-        high[k : k + 256, :] = a
-        low[k : k + 256, :] = b
+        for p in range(2):
+            for q in range(NZ // 2):
+                take = slice((2 * q + p) * CHUNK, (2 * q + p + 1) * CHUNK)
+                high[p, k : k + 256, q * CHUNK : (q + 1) * CHUNK] = a[:, take]
+                low[p, k : k + 256, q * CHUNK : (q + 1) * CHUNK] = b[:, take]
         a, b = halves(part.T)
         th[:, k : k + 256] = a
         tl[:, k : k + 256] = b
@@ -107,31 +110,57 @@
     out[row : row + 1, :] = jnp.full((1, BLOCK), (count * BLOCK).astype(F32))
 
 
-def cost_body(place, core, nblk, dblk, high, low, squares, *refs):
-    pieces, (cost, out, turned, data_high, data_low) = refs[:NZ], refs[NZ:]
+def neighbour(z):
+    return z + 1 - 2 * lax.rem(z, 2)
+
+
+def chunk_of(z, q):
+    return lax.rem(z + (NZ - 2 * q), NZ)
+
+
+def half_product(z, four, high, low, data_high, data_low):
     square = jnp.zeros((1, COLS), F32)
-    for s in range(NZ):
-        z = lax.rem(place[0] + (NZ - s), NZ)
-        piece = pieces[s][...]
+    for q in range(NZ // 2):
+        piece = four[q * CHUNK : (q + 1) * CHUNK, :]
         square += jnp.sum(piece * piece, axis=0, keepdims=True)
         a, b = halves(piece)
-        at = pl.multiple_of(z * CHUNK, CHUNK)
+        at = pl.multiple_of(lax.div(chunk_of(z, q), 2) * CHUNK, CHUNK)
         data_high[pl.ds(at, CHUNK), :] = a
         data_low[pl.ds(at, CHUNK), :] = b
-        for q in range(CHUNK // OWN):
-            to = pl.multiple_of((z * 2 + q // 2) * OWN, OWN)
-            turned[q % 2, 0, pl.ds(to, OWN), :] = a[q * OWN : (q + 1) * OWN]
-            turned[q % 2, 1, pl.ds(to, OWN), :] = b[q * OWN : (q + 1) * OWN]
+    both = (data_high[...], data_low[...])
+    side = lax.rem(z, 2)
+
+    def cross(k):
+        part = slice(k, k + 256)
+        return square - 2.0 * dot3((high[side, part, :], low[side, part, :]), both, ((1,), (0,)))
+
+    return cross
+
+
+def near_body(place, high, low, squares, four, cost, data_high, data_low):
+    cross = half_product(place[0], four, high, low, data_high, data_low)
+    for k in range(0, ROWS, 256):
+        cost[k : k + 256, :] = squares[k : k + 256, :] + cross(k)
+
+
+def cost_body(place, dblk, high, low, four, other, near, cost, out, turned, data_high, data_low):
+    z = place[0]
+    cross = half_product(neighbour(z), other, high, low, data_high, data_low)
     eye = diagonal()
     bias = jnp.where(live_columns(dblk), 0.0, -jnp.inf)
-    both = (data_high[...], data_low[...])
+    out[...] = jnp.zeros((LROWS, BLOCK), F32)
     for k in range(0, ROWS, 256):
-        cross = dot3((high[k : k + 256, :], low[k : k + 256, :]), both, ((1,), (0,)))
-        cost[k : k + 256, :] = SHARP * (squares[k : k + 256, :] + square - 2.0 * cross)
-    out[...] = jnp.zeros((LROWS, BLOCK), F32)
+        cost[k : k + 256, :] = SHARP * (near[k : k + 256, :] + cross(k))
     for k in range(RB):
         out[k : k + 1, :] = to_row(row_lse(cost, bias, k), eye)
     store_count(out, RB, dblk[0])
+    for source, came in ((z, four), (neighbour(z), other)):
+        for q in range(NZ // 2):
+            for h in range(CHUNK // OWN):
+                a, b = halves(came[q * CHUNK + h * OWN : q * CHUNK + (h + 1) * OWN, :])
+                to = pl.multiple_of((chunk_of(source, q) * 2 + h // 2) * OWN, OWN)
+                turned[h % 2, 0, pl.ds(to, OWN), :] = a
+                turned[h % 2, 1, pl.ds(to, OWN), :] = b
 
 
 def joined(values):
@@ -190,7 +219,7 @@
 
 
 def project_noise_body(place, nblk, own, dual, cost, turned_high, turned_low, *refs):
-    outs, (whole, th, tl, weights_high, weights_low, sems) = refs[:NZ], refs[NZ:]
+    stay, away, whole, th, tl, weights_high, weights_low, sems = refs
     copies = [
         pltpu.make_async_copy(turned_high, th, sems.at[0]),
         pltpu.make_async_copy(turned_low, tl, sems.at[1]),
@@ -215,10 +244,12 @@
                 whole[k // CHUNK + q, c * CHUNK : (c + 1) * CHUNK, :] = some[
                     q * CHUNK : (q + 1) * CHUNK, c * BLOCK : (c + 1) * BLOCK
                 ]
-    moves = [
-        pltpu.make_async_copy(whole.at[lax.rem(place[0] + s, NZ)], outs[s], sems.at[2 + s])
-        for s in range(NZ)
-    ]
+    z = place[0]
+    moves = []
+    for q in range(NZ // 2):
+        for n, (source, out) in enumerate(((neighbour(z), away), (z, stay))):
+            take = whole.at[lax.rem(source + 2 * q, NZ)]
+            moves.append(pltpu.make_async_copy(take, out.at[q], sems.at[2 + 2 * q + n]))
     for move in moves:
         move.start()
     for move in moves:
@@ -289,19 +320,26 @@
         out[:, k * BLOCK : (k + 1) * BLOCK] = jnp.where(k < nblk[0], total, 0.0)
 
 
-def finish_data_body(place, dblk, got, *refs):
-    came, out = refs[:NZ], refs[NZ]
+def pair_body(place, got, stay, came, *outs):
     level = joined(got[...])
-    shares = [jnp.exp(got[lax.rem(place[0] + (NZ - s), NZ)] - level) for s in range(NZ)]
+    a = jnp.exp(got[place[0]] - level)
+    b = jnp.exp(got[neighbour(place[0])] - level)
+    for q in range(NZ // 2):
+        for k in range(CB):
+            part = slice(k * CHUNK, (k + 1) * CHUNK)
+            outs[q][part, :] = stay[q, part, :] * a[k : k + 1, :] + came[q, part, :] * b[k : k + 1, :]
+
+
+def finish_data_body(dblk, *refs):
+    came, out = refs[: NZ // 2], refs[NZ // 2]
     for k in range(CB):
         part = slice(k * CHUNK, (k + 1) * CHUNK)
-        total = came[0][part, :] * shares[0][k : k + 1, :]
-        for s in range(1, NZ):
-            total += came[s][part, :] * shares[s][k : k + 1, :]
+        total = (came[0][part, :] + came[1][part, :]) + (came[2][part, :] + came[3][part, :])
         out[:, k * BLOCK : (k + 1) * BLOCK] = jnp.where(k < dblk[0], total, 0.0)
 
 
 CORES = [(0, 1), (1, 0)]
+PAIRS = [(i, i ^ 1) for i in range(NZ)]
 
 
 def over_dp(lse):
@@ -323,14 +361,16 @@
     place = lax.axis_index("z").reshape(1)
     core = lax.axis_index("c").reshape(1)
     mine, place, core = lax.optimization_barrier((data_points.T, place, core))
-    pieces = [mine] + [
-        lax.ppermute(mine, "z", [(i, (i + s) % NZ) for i in range(NZ)]) for s in range(1, NZ)
-    ]
+    four = jnp.concatenate(
+        [mine]
+        + [lax.ppermute(mine, "z", [(i, (i + 2 * q) % NZ) for i in range(NZ)]) for q in (1, 2, 3)]
+    )
+    other = lax.ppermute(four, "z", PAIRS)
     high, low, turned_high, turned_low, squares = call(
         prepare_body,
         (
-            shaped((ROWS, DIM), BF16),
-            shaped((ROWS, DIM), BF16),
+            shaped((2, ROWS, DIM // 2), BF16),
+            shaped((2, ROWS, DIM // 2), BF16),
             pltpu.HBM((DIM, ROWS), BF16),
             pltpu.HBM((DIM, ROWS), BF16),
             shaped((ROWS, 1)),
@@ -344,13 +384,20 @@
         limit=8,
         places=(VMEM, VMEM, HBM, HBM, VMEM),
     )(place, core, noise_blocks, data_blocks, noise_points)
+    near = call(
+        near_body,
+        shaped((ROWS, COLS)),
+        [SMEM] + [VMEM] * 4,
+        [pltpu.VMEM((DIM // 2, COLS), BF16), pltpu.VMEM((DIM // 2, COLS), BF16)],
+        limit=6,
+    )(place, high, low, squares, four)
     cost, lse, turned = call(
         cost_body,
         (shaped((ROWS, COLS)), shaped((LROWS, BLOCK)), shaped((NC, 2, DIM // NC, COLS), BF16)),
-        [SMEM] * 4 + [VMEM] * (3 + NZ),
-        [pltpu.VMEM((DIM, COLS), BF16), pltpu.VMEM((DIM, COLS), BF16)],
+        [SMEM, SMEM] + [VMEM] * 5,
+        [pltpu.VMEM((DIM // 2, COLS), BF16), pltpu.VMEM((DIM // 2, COLS), BF16)],
         limit=6,
-    )(place, core, noise_blocks, data_blocks, high, low, squares, *pieces)
+    )(place, data_blocks, high, low, four, other, near)
     for turn in range(ITERS):
         if turn:
             lse = call(row_body, shaped((LROWS, BLOCK)), [SMEM, VMEM, VMEM])(data_blocks, got, cost)
@@ -362,9 +409,9 @@
             [pltpu.VMEM((ROWS, 1), F32)],
         )(noise_blocks, rows, cost)
         got = over_noise(sent)
-    halfway = call(
+    stay, away = call(
         project_noise_body,
-        [pltpu.HBM((CB * CHUNK, BLOCK), F32) for _ in range(NZ)],
+        [pltpu.HBM((NZ // 2, CB * CHUNK, BLOCK), F32) for _ in range(2)],
         [SMEM, SMEM, VMEM, VMEM, VMEM, HBM, HBM],
         [
             pltpu.VMEM((NZ, CB * CHUNK, BLOCK), F32),
@@ -374,7 +421,7 @@
             pltpu.VMEM((ROWS, COLS), BF16),
             pltpu.SemaphoreType.DMA((2 + NZ,)),
         ],
-        places=[HBM] * NZ,
+        places=[HBM] * 2,
     )(
         place,
         noise_blocks,
@@ -384,10 +431,14 @@
         pltpu.with_memory_space_constraint(turned_high, pltpu.HBM),
         pltpu.with_memory_space_constraint(turned_low, pltpu.HBM),
     )
-    got, halfway = lax.optimization_barrier((got, halfway))
-    data_came = [halfway[0]] + [
-        lax.ppermute(halfway[s], "z", [(i, (i + s) % NZ) for i in range(NZ)])
-        for s in range(1, NZ)
+    got, stay, away = lax.optimization_barrier((got, stay, away))
+    paired = lax.ppermute(away, "z", PAIRS)
+    summed = call(
+        pair_body, [shaped((CB * CHUNK, BLOCK)) for _ in range(NZ // 2)], [SMEM, VMEM, VMEM, VMEM]
+    )(place, got, stay, paired)
+    data_came = [summed[0]] + [
+        lax.ppermute(summed[q], "z", [(i, (i + 2 * q) % NZ) for i in range(NZ)])
+        for q in (1, 2, 3)
     ]
     theirs, weights_high, weights_low, data_dual, level = call(
         project_data_body,
@@ -410,8 +461,8 @@
         noise_blocks, noise_came
     )
     data_target = call(
-        finish_data_body, shaped((CHUNK, COLS)), [SMEM, SMEM] + [VMEM] * (1 + NZ)
-    )(place, data_blocks, got, *data_came)
+        finish_data_body, shaped((CHUNK, COLS)), [SMEM] + [VMEM] * (NZ // 2)
+    )(data_blocks, *data_came)
     row_live = jnp.arange(ROWS, dtype=jnp.int32) < noise_blocks[0] * BLOCK
     column_live = jnp.arange(COLS, dtype=jnp.int32) < data_blocks[0] * BLOCK
     noise_potential = jnp.where(row_live, SMOOTHING_TEMP * dual[:RB].reshape(ROWS), 0.0)

time: 155 us -> 152 us (0.981)
  starting transfers between devices: 48.6 us -> 36.3 us
  waiting for transfers between devices: 23 us -> 29.6 us
  Pallas kernels: 24.1 us -> 25.7 us
    ppermute x14 -> x8, starting transfers between devices: 31.1 us -> 18.4 us  [the longest x3 11.4 us: on_device(): lax.ppermute(mine, 'z', [(i, (i + 2 * q) % NZ) for i in range(NZ)])]
    ppermute x14 -> x8, waiting for transfers between devices: 18.4 us -> 24.3 us  [the longest x1 9.39 us: on_device(): paired = lax.ppermute(away, 'z', PAIRS)]
    pallas_call x3 -> x5, Pallas kernels: 10.4 us -> 13.2 us  [the longest x1 6.44 us: on_device(): call(project_noise_body, [pltpu.HBM((NZ // 2, CB * CHUNK, BLOCK), F32) fo...]
  transfers between devices with their start and end apart: 20 -> 14, of which waited for: 12 -> 12; matrix products, arithmetic and copies ran while one was open for 1% -> 1% of each run, Pallas kernels for 8% -> 10%
where the time goes in v3:
time: 152 us
  blocking collectives  53.6 us (35%)
  starting transfers between devices  36.3 us (24%)
  waiting for transfers between devices  29.6 us (19%)
  Pallas kernels  25.7 us (17%)
  local copies, waits for them, and re-layouts  2.89 us (2%)
  between operations  2.11 us (1%)
    all_to_all x3, blocking collectives, over_dp(): lax.all_to_all(jnp.broadcast_to(both[None], (NXY, LROWS, BLOCK)), ('x', '...  32.9 us
    all_to_all x2, blocking collectives, over_noise(): return lax.all_to_all(pieces, 'z', 0, 0, tiled=True)  20.8 us
    ppermute x3, starting transfers between devices, on_device(): lax.ppermute(mine, 'z', [(i, (i + 2 * q) % NZ) for i in range(NZ)])  11.4 us
    ppermute x1, waiting for transfers between devices, on_device(): paired = lax.ppermute(away, 'z', PAIRS)  9.39 us
    ppermute x3, starting transfers between devices, over_dp(): came = lax.ppermute(lse, 'c', CORES)  7.74 us
    ppermute x3, waiting for transfers between devices, on_device(): lax.ppermute(mine, 'z', [(i, (i + 2 * q) % NZ) for i in range(NZ)])  6.99 us
    ppermute x3, waiting for transfers between devices, on_device(): lax.ppermute(summed[q], 'z', [(i, (i + 2 * q) % NZ) for i in range(NZ)])  6.97 us
    ppermute x3, starting transfers between devices, on_device(): lax.ppermute(summed[q], 'z', [(i, (i + 2 * q) % NZ) for i in range(NZ)])  6.53 us
  transfers between devices with their start and end apart: 14, of which 12 were waited for; matrix products, arithmetic and copies ran while one was open for 1% of the time, Pallas kernels for 10%

profile of v3, /device:TPU:1, one launch (start us, length us, event | category | flops | bytes accessed | tf_op | source)
XLA Modules:
  0.0 151.7 jit_solution(14685705082432802789)
XLA Ops:
  0.6 3.9 %collective-permute-start = (f32[64,384]{1,0:T(8,128)}, f32[64,384]{1,0:T(8,128)S(1)}, u32[]{:S(2)}, u32[]{:S(2)}) collective-permute-start(f32[64,384]{1,0:T(8,128)} %bitcast.7), channel_id=1, source_target_pairs={{0,64},{32,96},{64,128},{96,160},{128,192},{160,224},{192,0},{224,... | collective-permute-start | bytes 294920 | tf_op jit(solution)/shard_map/ppermute | solution.py:366
  4.5 5.1 %collective-permute-start.1 = (f32[64,384]{1,0:T(8,128)}, f32[64,384]{1,0:T(8,128)S(1)}, u32[]{:S(2)}, u32[]{:S(2)}) collective-permute-start(f32[64,384]{1,0:T(8,128)} %bitcast.8), channel_id=1, source_target_pairs={{0,128},{32,160},{64,192},{96,224},{128,0},{160,32},{192,64},{224,... | collective-permute-start | bytes 294920 | tf_op jit(solution)/shard_map/ppermute | solution.py:366
  9.6 2.4 %collective-permute-start.2 = (f32[64,384]{1,0:T(8,128)}, f32[64,384]{1,0:T(8,128)S(1)}, u32[]{:S(2)}, u32[]{:S(2)}) collective-permute-start(f32[64,384]{1,0:T(8,128)} %bitcast.9), channel_id=1, source_target_pairs={{0,192},{32,224},{64,0},{96,32},{128,64},{160,96},{192,128},{224,1... | collective-permute-start | bytes 294920 | tf_op jit(solution)/shard_map/ppermute | solution.py:366
  12.0 0.9 constant_dynamic-update-slice_fusion.3
  13.0 0.0 collective-permute-done
  13.0 3.1 %collective-permute-done.1 = f32[64,384]{1,0:T(8,128)S(1)} collective-permute-done((f32[64,384]{1,0:T(8,128)}, f32[64,384]{1,0:T(8,128)S(1)}, u32[]{:S(2)}, u32[]{:S(2)}) %collective-permute-start.1) | collective-permute-done | bytes 98336 | tf_op jit(solution)/shard_map/ppermute | solution.py:366
  16.1 3.9 %collective-permute-done.2 = f32[64,384]{1,0:T(8,128)S(1)} collective-permute-done((f32[64,384]{1,0:T(8,128)}, f32[64,384]{1,0:T(8,128)S(1)}, u32[]{:S(2)}, u32[]{:S(2)}) %collective-permute-start.2) | collective-permute-done | bytes 98336 | tf_op jit(solution)/shard_map/ppermute | solution.py:366
  20.0 0.1 collective-permute-start.3
  21.4 0.0 copy-start
  21.4 1.9 %copy-done = f32[1536,512]{1,0:T(8,128)S(1)} copy-done((f32[1536,512]{1,0:T(8,128)S(1)}, f32[1536,512]{1,0:T(8,128)}, u32[]{:S(2)}) %copy-start) | copy-done | bytes 3145752
  23.3 4.6 %shard_map.75 = (bf16[2,1536,256]{2,1,0:T(8,128)(2,1)S(1)}, bf16[2,1536,256]{2,1,0:T(8,128)(2,1)S(1)}, bf16[512,1536]{1,0:T(8,128)(2,1)}, bf16[512,1536]{1,0:T(8,128)(2,1)}, f32[1536,1]{1,0:T(8,128)S(1)}) custom-call(s32[1]{0:T(128)} %bitcast.2.place, s32[1]{0:T(128)} %bitcast.3.core, s32[1]{0:T(128)S(6)} %copy.11.nblk, s32[1]{0:T(128)S(6)} %copy.12.dblk, ...), custom_call_target="tpu_custom_call" | custom-call | flops 1000000 | bytes 4000000 | tf_op jit(solution)/shard_map/pallas_call | solution.py:369
  27.8 1.5 shard_map.76.near
  29.3 0.9 collective-permute-done.3.other
  30.3 1.9 %shard_map.77 = (f32[1536,384]{1,0:T(8,128)S(1)}, f32[16,128]{1,0:T(8,128)S(1)}, bf16[2,2,256,384]{3,2,1,0:T(8,128)(2,1)S(1)}) custom-call(s32[1]{0:T(128)} %bitcast.2.place, s32[1]{0:T(128)S(6)} %copy.12.dblk, bf16[2,1536,256]{2,1,0:T(8,128)(2,1)S(1)} %get-tuple-element.35.high, bf16[2,1536,256]{2,1,0:T(8,128)(2,1)S(1)} %get-tuple-element.36.low, ...), custom_call_target="tpu_custom_call" | custom-call | flops 1000000 | bytes 4000000 | tf_op jit(solution)/shard_map/pallas_call | solution.py:394
  32.2 1.4 collective-permute-start.4
  33.6 0.8 collective-permute-done.4
  34.4 0.1 add_select_fusion.2
  34.5 13.2 %all_to_all.35.got = f32[16,16,128]{2,1,0:T(8,128)S(1)} all-to-all(f32[16,16,128]{2,1,0:T(8,128)S(1)} %broadcast_in_dim.12), channel_id=1, replica_groups=mesh['z'=8,'x'=4,'y'=4,'c'=2] {'x','y'}, dimensions={0} | all-to-all | bytes 262144 | tf_op jit(solution)/shard_map/all_to_all | solution.py:351
  47.8 0.8 shard_map.78
  48.6 11.5 %all_to_all.36.got = f32[8,8,128]{2,1,0:T(8,128)S(1)} all-to-all(f32[8,8,128]{2,1,0:T(8,128)S(1)} %get-tuple-element.41), channel_id=1, replica_groups=mesh['z'=8,'x'=4,'y'=4,'c'=2] {'z'}, dimensions={0} | all-to-all | bytes 65536 | tf_op jit(solution)/shard_map/all_to_all | solution.py:357
  60.1 1.0 shard_map.79
  61.1 3.3 %collective-permute-start.5 = (f32[16,128]{1,0:T(8,128)S(1)}, f32[16,128]{1,0:T(8,128)S(1)}, u32[]{:S(2)}, u32[]{:S(2)}) collective-permute-start(f32[16,128]{1,0:T(8,128)S(1)} %shard_map.79), channel_id=1, source_target_pairs={{0,1},{1,0},{2,3},{3,2},{4,5},{5,4},{6,7},{7,6},{8,9},{9,8},{10,11... | collective-permute-start | bytes 24584 | tf_op jit(solution)/shard_map/ppermute | solution.py:346
  64.4 0.8 collective-permute-done.5
  65.2 0.1 add_select_fusion.1
  65.3 9.8 %all_to_all.37.got = f32[16,16,128]{2,1,0:T(8,128)S(1)} all-to-all(f32[16,16,128]{2,1,0:T(8,128)S(1)} %broadcast_in_dim.14), channel_id=1, replica_groups=mesh['z'=8,'x'=4,'y'=4,'c'=2] {'x','y'}, dimensions={0} | all-to-all | bytes 262144 | tf_op jit(solution)/shard_map/all_to_all | solution.py:351
  75.1 0.8 shard_map.80
  75.9 9.2 %all_to_all.38.got = f32[8,8,128]{2,1,0:T(8,128)S(1)} all-to-all(f32[8,8,128]{2,1,0:T(8,128)S(1)} %get-tuple-element.42), channel_id=1, replica_groups=mesh['z'=8,'x'=4,'y'=4,'c'=2] {'z'}, dimensions={0} | all-to-all | bytes 65536 | tf_op jit(solution)/shard_map/all_to_all | solution.py:357
  85.2 1.0 shard_map.81
  86.2 3.0 %collective-permute-start.6 = (f32[16,128]{1,0:T(8,128)S(1)}, f32[16,128]{1,0:T(8,128)S(1)}, u32[]{:S(2)}, u32[]{:S(2)}) collective-permute-start(f32[16,128]{1,0:T(8,128)S(1)} %shard_map.81), channel_id=1, source_target_pairs={{0,1},{1,0},{2,3},{3,2},{4,5},{5,4},{6,7},{7,6},{8,9},{9,8},{10,11... | collective-permute-start | bytes 24584 | tf_op jit(solution)/shard_map/ppermute | solution.py:346
  89.2 0.8 collective-permute-done.6
  90.0 0.1 add_select_fusion
  90.1 9.8 %all_to_all.39.got = f32[16,16,128]{2,1,0:T(8,128)S(1)} all-to-all(f32[16,16,128]{2,1,0:T(8,128)S(1)} %broadcast_in_dim.28), channel_id=1, replica_groups=mesh['z'=8,'x'=4,'y'=4,'c'=2] {'x','y'}, dimensions={0} | all-to-all | bytes 262144 | tf_op jit(solution)/shard_map/all_to_all | solution.py:351
  99.9 1.4 shard_map.82
  101.3 3.3 %all-to-all-start.5 = ((f32[8,8,128]{2,1,0:T(8,128)}), f32[8,8,128]{2,1,0:T(8,128)S(1)}, u32[]{:S(2)}, u32[]{:S(2)}) async-start(f32[8,8,128]{2,1,0:T(8,128)} %get-tuple-element.44.own), calls=%async_computation.5 | async-start | bytes 65536 | tf_op jit(solution)/shard_map/all_to_all | solution.py:357
  104.6 6.4 %shard_map.83 = (f32[4,192,128]{2,1,0:T(8,128)}, f32[4,192,128]{2,1,0:T(8,128)}) custom-call(s32[1]{0:T(128)} %bitcast.2.place, s32[1]{0:T(128)S(6)} %copy.11.nblk, f32[8,8,128]{2,1,0:T(8,128)} %get-tuple-element.44.own, f32[16,128]{1,0:T(8,128)S(1)} %get-tuple-element.43.dual, f32[1536,384]{1,0:T(8,128)S(1)} %get-tuple-element.40.cost, ...), custom_call_target="tpu_custom_call" | custom-call | flops 1000000 | bytes 4000000 | tf_op jit(solution)/shard_map/pallas_call | solution.py:412
  111.1 0.3 all-to-all-done.5.got
  111.4 1.9 %shard_map.84 = (f32[16,216,128]{2,1,0:T(8,128)S(1)}, bf16[1536,384]{1,0:T(8,128)(2,1)S(1)}, bf16[1536,384]{1,0:T(8,128)(2,1)S(1)}, f32[1,384]{1,0:T(1,128)S(1)}, f32[24,128]{1,0:T(8,128)S(1)}) custom-call(s32[1]{0:T(128)} %bitcast.3.core, s32[1]{0:T(128)S(6)} %copy.12.dblk, f32[8,8,128]{2,1,0:T(8,128)S(1)} %all-to-all-done.5.got, ...), custom_call_target="tpu_custom_call" | custom-call | flops 1000000 | bytes 4000000 | tf_op jit(solution)/shard_map/pallas_call | solution.py:443
  113.4 3.0 %collective-permute-start.7 = (f32[16,216,128]{2,1,0:T(8,128)S(1)}, f32[16,216,128]{2,1,0:T(8,128)S(1)}, u32[]{:S(2)}, u32[]{:S(2)}) collective-permute-start(f32[16,216,128]{2,1,0:T(8,128)S(1)} %get-tuple-element.55), channel_id=1, source_target_pairs={{0,1},{1,0},{2,3},{3,2},{4,5},{5,4},{6,7},{7,6},{8,9},{9,8},{10,11... | collective-permute-start | bytes 5308424 | tf_op jit(solution)/shard_map/ppermute | solution.py:454
  116.4 1.4 shard_map.85.own
  117.8 1.9 %collective-permute-done.7.came = f32[16,216,128]{2,1,0:T(8,128)S(1)} collective-permute-done((f32[16,216,128]{2,1,0:T(8,128)S(1)}, f32[16,216,128]{2,1,0:T(8,128)S(1)}, u32[]{:S(2)}, u32[]{:S(2)}) %collective-permute-start.7) | collective-permute-done | bytes 1769504 | tf_op jit(solution)/shard_map/ppermute | solution.py:454
  119.7 1.4 shard_map.86
  121.1 0.0 copy-start.2
  121.1 0.0 copy-start.1
  121.1 3.8 %all-to-all-start.6 = ((f32[16,216,128]{2,1,0:T(8,128)}), f32[16,216,128]{2,1,0:T(8,128)S(1)}, u32[]{:S(2)}, u32[]{:S(2)}) async-start(f32[16,216,128]{2,1,0:T(8,128)} %shard_map.86), calls=%async_computation.6 | async-start | bytes 3538944 | tf_op jit(solution)/shard_map/all_to_all | solution.py:459
  125.0 0.0 copy-done.2
  125.0 0.4 collective-permute-start.8
  125.4 0.6 bitcast_select_fusion
  126.0 9.4 %collective-permute-done.8.came = f32[4,192,128]{2,1,0:T(8,128)S(1)} collective-permute-done((f32[4,192,128]{2,1,0:T(8,128)S(1)}, f32[4,192,128]{2,1,0:T(8,128)S(1)}, u32[]{:S(2)}, u32[]{:S(2)}) %collective-permute-start.8) | collective-permute-done | bytes 393248 | tf_op jit(solution)/shard_map/ppermute | solution.py:435
  135.4 0.0 copy-done.1
  135.4 0.1 shard_map.88
  135.5 4.2 %collective-permute-start.10 = (f32[192,128]{1,0:T(8,128)S(1)}, f32[192,128]{1,0:T(8,128)S(1)}, u32[]{:S(2)}, u32[]{:S(2)}) collective-permute-start(f32[192,128]{1,0:T(8,128)S(1)} %get-tuple-element.60), channel_id=1, source_target_pairs={{0,128},{32,160},{64,192},{96,224},{128,0},{160,32},{192,64},{224,... | collective-permute-start | bytes 294920 | tf_op jit(solution)/shard_map/ppermute | solution.py:440
  139.7 0.3 collective-permute-start.11
  139.9 2.1 %collective-permute-start.9 = (f32[192,128]{1,0:T(8,128)S(1)}, f32[192,128]{1,0:T(8,128)S(1)}, u32[]{:S(2)}, u32[]{:S(2)}) collective-permute-start(f32[192,128]{1,0:T(8,128)S(1)} %get-tuple-element.59), channel_id=1, source_target_pairs={{0,64},{32,96},{64,128},{96,160},{128,192},{160,224},{192,0},{224,... | collective-permute-start | bytes 294920 | tf_op jit(solution)/shard_map/ppermute | solution.py:440
  142.0 0.6 fusion.3
  142.6 0.4 collective-permute-done.10.refs_2_
  143.0 6.5 %collective-permute-done.11.refs_3_ = f32[192,128]{1,0:T(8,128)S(1)} collective-permute-done((f32[192,128]{1,0:T(8,128)S(1)}, f32[192,128]{1,0:T(8,128)S(1)}, u32[]{:S(2)}, u32[]{:S(2)}) %collective-permute-start.11) | collective-permute-done | bytes 98336 | tf_op jit(solution)/shard_map/ppermute | solution.py:440
  149.6 0.0 collective-permute-done.9.refs_1_
  149.6 0.7 shard_map.89
  150.2 0.6 all-to-all-done.6.came
  150.8 0.9 shard_map.87
  (8 shorter events, 0.1 us)
Async XLA Ops:
  0.6 12.3 %collective-permute-start = (f32[64,384]{1,0:T(8,128)}, f32[64,384]{1,0:T(8,128)S(1)}, u32[]{:S(2)}, u32[]{:S(2)}) collective-permute-start(f32[64,384]{1,0:T(8,128)} %bitcast.7), channel_id=1, source_target_pairs={{0,64},{32,96},{64,128},{96,160},{128,192},{160,224},{192,0},{224,... | collective-permute-start | bytes 294920 | tf_op jit(solution)/shard_map/ppermute | solution.py:366
  4.5 11.5 %collective-permute-start.1 = (f32[64,384]{1,0:T(8,128)}, f32[64,384]{1,0:T(8,128)S(1)}, u32[]{:S(2)}, u32[]{:S(2)}) collective-permute-start(f32[64,384]{1,0:T(8,128)} %bitcast.8), channel_id=1, source_target_pairs={{0,128},{32,160},{64,192},{96,224},{128,0},{160,32},{192,64},{224,... | collective-permute-start | bytes 294920 | tf_op jit(solution)/shard_map/ppermute | solution.py:366
  9.6 10.3 %collective-permute-start.2 = (f32[64,384]{1,0:T(8,128)}, f32[64,384]{1,0:T(8,128)S(1)}, u32[]{:S(2)}, u32[]{:S(2)}) collective-permute-start(f32[64,384]{1,0:T(8,128)} %bitcast.9), channel_id=1, source_target_pairs={{0,192},{32,224},{64,0},{96,32},{128,64},{160,96},{192,128},{224,1... | collective-permute-start | bytes 294920 | tf_op jit(solution)/shard_map/ppermute | solution.py:366
  20.0 10.3 %collective-permute-start.3 = (f32[256,384]{1,0:T(8,128)S(1)}, f32[256,384]{1,0:T(8,128)S(1)}, u32[]{:S(2)}, u32[]{:S(2)}) collective-permute-start(f32[256,384]{1,0:T(8,128)S(1)} %constant_dynamic-update-slice_fusion.four), channel_id=1, source_target_pairs={{0,32},{32,0},{64,96},{96,64},{128,160},{160,128},{192,224},{224,1... | collective-permute-start | bytes 1179656 | tf_op jit(solution)/shard_map/ppermute | solution.py:368
  21.4 1.9 %copy-start = (f32[1536,512]{1,0:T(8,128)S(1)}, f32[1536,512]{1,0:T(8,128)}, u32[]{:S(2)}) copy-start(f32[1536,512]{1,0:T(8,128)} %points.1) | copy-start | bytes 9437188
  32.2 2.3 %collective-permute-start.4 = (f32[16,128]{1,0:T(8,128)S(1)}, f32[16,128]{1,0:T(8,128)S(1)}, u32[]{:S(2)}, u32[]{:S(2)}) collective-permute-start(f32[16,128]{1,0:T(8,128)S(1)} %get-tuple-element.39), channel_id=1, source_target_pairs={{0,1},{1,0},{2,3},{3,2},{4,5},{5,4},{6,7},{7,6},{8,9},{9,8},{10,11... | collective-permute-start | bytes 24584 | tf_op jit(solution)/shard_map/ppermute | solution.py:346
  61.1 4.1 %collective-permute-start.5 = (f32[16,128]{1,0:T(8,128)S(1)}, f32[16,128]{1,0:T(8,128)S(1)}, u32[]{:S(2)}, u32[]{:S(2)}) collective-permute-start(f32[16,128]{1,0:T(8,128)S(1)} %shard_map.79), channel_id=1, source_target_pairs={{0,1},{1,0},{2,3},{3,2},{4,5},{5,4},{6,7},{7,6},{8,9},{9,8},{10,11... | collective-permute-start | bytes 24584 | tf_op jit(solution)/shard_map/ppermute | solution.py:346
  86.2 3.8 %collective-permute-start.6 = (f32[16,128]{1,0:T(8,128)S(1)}, f32[16,128]{1,0:T(8,128)S(1)}, u32[]{:S(2)}, u32[]{:S(2)}) collective-permute-start(f32[16,128]{1,0:T(8,128)S(1)} %shard_map.81), channel_id=1, source_target_pairs={{0,1},{1,0},{2,3},{3,2},{4,5},{5,4},{6,7},{7,6},{8,9},{9,8},{10,11... | collective-permute-start | bytes 24584 | tf_op jit(solution)/shard_map/ppermute | solution.py:346
  101.3 10.1 %all-to-all-start.5 = ((f32[8,8,128]{2,1,0:T(8,128)}), f32[8,8,128]{2,1,0:T(8,128)S(1)}, u32[]{:S(2)}, u32[]{:S(2)}) async-start(f32[8,8,128]{2,1,0:T(8,128)} %get-tuple-element.44.own), calls=%async_computation.5 | async-start | bytes 65536 | tf_op jit(solution)/shard_map/all_to_all | solution.py:357
  113.4 6.3 %collective-permute-start.7 = (f32[16,216,128]{2,1,0:T(8,128)S(1)}, f32[16,216,128]{2,1,0:T(8,128)S(1)}, u32[]{:S(2)}, u32[]{:S(2)}) collective-permute-start(f32[16,216,128]{2,1,0:T(8,128)S(1)} %get-tuple-element.55), channel_id=1, source_target_pairs={{0,1},{1,0},{2,3},{3,2},{4,5},{5,4},{6,7},{7,6},{8,9},{9,8},{10,11... | collective-permute-start | bytes 5308424 | tf_op jit(solution)/shard_map/ppermute | solution.py:454
  121.1 3.9 %copy-start.2 = (f32[4,192,128]{2,1,0:T(8,128)S(1)}, f32[4,192,128]{2,1,0:T(8,128)}, u32[]{:S(2)}) copy-start(f32[4,192,128]{2,1,0:T(8,128)} %get-tuple-element.57) | copy-start | bytes 1179652
  121.1 14.3 %copy-start.1 = (f32[4,192,128]{2,1,0:T(8,128)S(1)}, f32[4,192,128]{2,1,0:T(8,128)}, u32[]{:S(2)}) copy-start(f32[4,192,128]{2,1,0:T(8,128)} %get-tuple-element.56.stay) | copy-start | bytes 1179652
  121.1 29.7 %all-to-all-start.6 = ((f32[16,216,128]{2,1,0:T(8,128)}), f32[16,216,128]{2,1,0:T(8,128)S(1)}, u32[]{:S(2)}, u32[]{:S(2)}) async-start(f32[16,216,128]{2,1,0:T(8,128)} %shard_map.86), calls=%async_computation.6 | async-start | bytes 3538944 | tf_op jit(solution)/shard_map/all_to_all | solution.py:459
  125.0 10.4 %collective-permute-start.8 = (f32[4,192,128]{2,1,0:T(8,128)S(1)}, f32[4,192,128]{2,1,0:T(8,128)S(1)}, u32[]{:S(2)}, u32[]{:S(2)}) collective-permute-start(f32[4,192,128]{2,1,0:T(8,128)S(1)} %copy-done.2), channel_id=1, source_target_pairs={{0,32},{32,0},{64,96},{96,64},{128,160},{160,128},{192,224},{224,1... | collective-permute-start | bytes 1179656 | tf_op jit(solution)/shard_map/ppermute | solution.py:435
  135.5 7.5 %collective-permute-start.10 = (f32[192,128]{1,0:T(8,128)S(1)}, f32[192,128]{1,0:T(8,128)S(1)}, u32[]{:S(2)}, u32[]{:S(2)}) collective-permute-start(f32[192,128]{1,0:T(8,128)S(1)} %get-tuple-element.60), channel_id=1, source_target_pairs={{0,128},{32,160},{64,192},{96,224},{128,0},{160,32},{192,64},{224,... | collective-permute-start | bytes 294920 | tf_op jit(solution)/shard_map/ppermute | solution.py:440
  139.7 9.9 %collective-permute-start.11 = (f32[192,128]{1,0:T(8,128)S(1)}, f32[192,128]{1,0:T(8,128)S(1)}, u32[]{:S(2)}, u32[]{:S(2)}) collective-permute-start(f32[192,128]{1,0:T(8,128)S(1)} %get-tuple-element.61), channel_id=1, source_target_pairs={{0,192},{32,224},{64,0},{96,32},{128,64},{160,96},{192,128},{224,1... | collective-permute-start | bytes 294920 | tf_op jit(solution)/shard_map/ppermute | solution.py:440
  139.9 9.6 %collective-permute-start.9 = (f32[192,128]{1,0:T(8,128)S(1)}, f32[192,128]{1,0:T(8,128)S(1)}, u32[]{:S(2)}, u32[]{:S(2)}) collective-permute-start(f32[192,128]{1,0:T(8,128)S(1)} %get-tuple-element.59), channel_id=1, source_target_pairs={{0,64},{32,96},{64,128},{96,160},{128,192},{160,224},{192,0},{224,... | collective-permute-start | bytes 294920 | tf_op jit(solution)/shard_map/ppermute | solution.py:440

commit v4 on v3

--- a/solution.py
+++ b/solution.py
@@ -22,6 +22,7 @@
 TOPS = RB * OWN
 LEVELS = TOPS + RB
 PIECE = TOPS + 2 * RB
+SENT = TOPS + LROWS
 
 SMEM = pl.BlockSpec(memory_space=pltpu.SMEM)
 VMEM = pl.BlockSpec(memory_space=pltpu.VMEM)
@@ -114,21 +115,27 @@
     return z + 1 - 2 * lax.rem(z, 2)
 
 
-def chunk_of(z, q):
-    return lax.rem(z + (NZ - 2 * q), NZ)
-
-
-def half_product(z, four, high, low, data_high, data_low):
+def near_pieces(z, refs):
+    return [(lax.rem(z + (NZ - 2 * q), NZ), refs[q][...]) for q in range(NZ // 2)]
+
+
+def far_pieces(z, left, right):
+    return [
+        (lax.rem(z + shift, NZ), side[h * CHUNK : (h + 1) * CHUNK, :])
+        for side, shifts in ((left, (NZ - 1, NZ - 3)), (right, (1, 3)))
+        for h, shift in enumerate(shifts)
+    ]
+
+
+def half_product(side, pieces, high, low, data_high, data_low):
     square = jnp.zeros((1, COLS), F32)
-    for q in range(NZ // 2):
-        piece = four[q * CHUNK : (q + 1) * CHUNK, :]
+    for source, piece in pieces:
         square += jnp.sum(piece * piece, axis=0, keepdims=True)
         a, b = halves(piece)
-        at = pl.multiple_of(lax.div(chunk_of(z, q), 2) * CHUNK, CHUNK)
+        at = pl.multiple_of(lax.div(source, 2) * CHUNK, CHUNK)
         data_high[pl.ds(at, CHUNK), :] = a
         data_low[pl.ds(at, CHUNK), :] = b
     both = (data_high[...], data_low[...])
-    side = lax.rem(z, 2)
 
     def cross(k):
         part = slice(k, k + 256)
@@ -137,15 +144,26 @@
     return cross
 
 
-def near_body(place, high, low, squares, four, cost, data_high, data_low):
-    cross = half_product(place[0], four, high, low, data_high, data_low)
+def turn(turned, pieces):
+    for source, piece in pieces:
+        for h in range(CHUNK // OWN):
+            a, b = halves(piece[h * OWN : (h + 1) * OWN, :])
+            to = pl.multiple_of((source * 2 + h // 2) * OWN, OWN)
+            turned[h % 2, 0, pl.ds(to, OWN), :] = a
+            turned[h % 2, 1, pl.ds(to, OWN), :] = b
+
+
+def near_body(place, high, low, squares, *refs):
+    pieces, (cost, data_high, data_low) = near_pieces(place[0], refs[:4]), refs[4:]
+    cross = half_product(lax.rem(place[0], 2), pieces, high, low, data_high, data_low)
     for k in range(0, ROWS, 256):
         cost[k : k + 256, :] = squares[k : k + 256, :] + cross(k)
 
 
-def cost_body(place, dblk, high, low, four, other, near, cost, out, turned, data_high, data_low):
-    z = place[0]
-    cross = half_product(neighbour(z), other, high, low, data_high, data_low)
+def cost_body(place, dblk, high, low, near, left, right, *refs):
+    z, own, (cost, out, turned, data_high, data_low) = place[0], refs[:4], refs[4:]
+    pieces = far_pieces(z, left, right)
+    cross = half_product(1 - lax.rem(z, 2), pieces, high, low, data_high, data_low)
     eye = diagonal()
     bias = jnp.where(live_columns(dblk), 0.0, -jnp.inf)
     out[...] = jnp.zeros((LROWS, BLOCK), F32)
@@ -154,13 +172,7 @@
     for k in range(RB):
         out[k : k + 1, :] = to_row(row_lse(cost, bias, k), eye)
     store_count(out, RB, dblk[0])
-    for source, came in ((z, four), (neighbour(z), other)):
-        for q in range(NZ // 2):
-            for h in range(CHUNK // OWN):
-                a, b = halves(came[q * CHUNK + h * OWN : q * CHUNK + (h + 1) * OWN, :])
-                to = pl.multiple_of((chunk_of(source, q) * 2 + h // 2) * OWN, OWN)
-                turned[h % 2, 0, pl.ds(to, OWN), :] = a
-                turned[h % 2, 1, pl.ds(to, OWN), :] = b
+    turn(turned, pieces + near_pieces(z, own))
 
 
 def joined(values):
@@ -307,12 +319,12 @@
             own[:, part, :] * a[k : k + 1, :][None] + came[:, part, :] * b[k : k + 1, :][None]
         )
     for p in range(NXY):
-        out[p, LEVELS:PIECE, :] = level
-        out[p, TOPS:LEVELS, :] = level
+        out[p, TOPS : TOPS + RB, :] = level
+        out[p, TOPS + RB : SENT, :] = level[0 : SENT - TOPS - RB, :]
 
 
 def finish_noise_body(nblk, came, out):
-    levels = came[:, LEVELS:PIECE, :]
+    levels = came[:, TOPS : TOPS + RB, :]
     shares = jnp.exp(levels - joined(levels)[None])
     for k in range(RB):
         part = slice(k * OWN, (k + 1) * OWN)
@@ -342,6 +354,10 @@
 PAIRS = [(i, i ^ 1) for i in range(NZ)]
 
 
+def shifted(s):
+    return [(i, (i + s) % NZ) for i in range(NZ)]
+
+
 def over_dp(lse):
     came = lax.ppermute(lse, "c", CORES)
     top = jnp.maximum(lse, came)
@@ -361,11 +377,9 @@
     place = lax.axis_index("z").reshape(1)
     core = lax.axis_index("c").reshape(1)
     mine, place, core = lax.optimization_barrier((data_points.T, place, core))
-    four = jnp.concatenate(
-        [mine]
-        + [lax.ppermute(mine, "z", [(i, (i + 2 * q) % NZ) for i in range(NZ)]) for q in (1, 2, 3)]
-    )
-    other = lax.ppermute(four, "z", PAIRS)
+    own = [mine] + [lax.ppermute(mine, "z", shifted(2 * q)) for q in (1, 2, 3)]
+    left = lax.ppermute(jnp.concatenate([mine, own[1]]), "z", shifted(1))
+    right = lax.ppermute(jnp.concatenate([mine, own[3]]), "z", shifted(NZ - 1))
     high, low, turned_high, turned_low, squares = call(
         prepare_body,
         (
@@ -387,17 +401,17 @@
     near = call(
         near_body,
         shaped((ROWS, COLS)),
-        [SMEM] + [VMEM] * 4,
+        [SMEM] + [VMEM] * 7,
         [pltpu.VMEM((DIM // 2, COLS), BF16), pltpu.VMEM((DIM // 2, COLS), BF16)],
         limit=6,
-    )(place, high, low, squares, four)
+    )(place, high, low, squares, *own)
     cost, lse, turned = call(
         cost_body,
         (shaped((ROWS, COLS)), shaped((LROWS, BLOCK)), shaped((NC, 2, DIM // NC, COLS), BF16)),
-        [SMEM, SMEM] + [VMEM] * 5,
+        [SMEM, SMEM] + [VMEM] * 9,
         [pltpu.VMEM((DIM // 2, COLS), BF16), pltpu.VMEM((DIM // 2, COLS), BF16)],
         limit=6,
-    )(place, data_blocks, high, low, four, other, near)
+    )(place, data_blocks, high, low, near, left, right, *own)
     for turn in range(ITERS):
         if turn:
             lse = call(row_body, shaped((LROWS, BLOCK)), [SMEM, VMEM, VMEM])(data_blocks, got, cost)
@@ -435,10 +449,14 @@
     paired = lax.ppermute(away, "z", PAIRS)
     summed = call(
         pair_body, [shaped((CB * CHUNK, BLOCK)) for _ in range(NZ // 2)], [SMEM, VMEM, VMEM, VMEM]
-    )(place, got, stay, paired)
+    )(
+        place,
+        got,
+        pltpu.with_memory_space_constraint(stay, pltpu.HBM),
+        pltpu.with_memory_space_constraint(paired, pltpu.HBM),
+    )
     data_came = [summed[0]] + [
-        lax.ppermute(summed[q], "z", [(i, (i + 2 * q) % NZ) for i in range(NZ)])
-        for q in (1, 2, 3)
+        lax.ppermute(summed[q], "z", shifted(2 * q)) for q in (1, 2, 3)
     ]
     theirs, weights_high, weights_low, data_dual, level = call(
         project_data_body,
@@ -455,7 +473,7 @@
     own = call(
         project_own_body, shaped((NXY, RB * OWN, BLOCK)), [SMEM, VMEM, VMEM, VMEM]
     )(core, turned, weights_high, weights_low)
-    merged = call(merge_body, shaped((NXY, PIECE, BLOCK)), [VMEM] * 3)(own, level, came)
+    merged = call(merge_body, pltpu.VMEM((NXY, SENT, BLOCK), F32), [VMEM] * 3)(own, level, came)
     noise_came = lax.all_to_all(merged, ("x", "y"), 0, 0, tiled=True)
     noise_target = call(finish_noise_body, shaped((OWN, ROWS)), [SMEM, VMEM])(
         noise_blocks, noise_came

time: 152 us -> 154 us (1.013)
  starting transfers between devices: 36.3 us -> 39.8 us
  waiting for transfers between devices: 29.6 us -> 27.4 us
    ppermute x7 -> x8, starting transfers between devices: 18 us -> 21 us  [the longest x3 10.5 us: on_device(): own = [mine] + [lax.ppermute(mine, 'z', shifted(2 * q)) for q in (1, 2, 3)]]
    ppermute x7 -> x8, waiting for transfers between devices: 14.9 us -> 13.3 us  [the longest x3 7.01 us: on_device(): lax.ppermute(summed[q], 'z', shifted(2 * q))]
  transfers between devices with their start and end apart: 14 -> 15, of which waited for: 12 -> 10; matrix products, arithmetic and copies ran while one was open for 1% -> 1% of each run, Pallas kernels for 10% -> 10%
where the time goes in v4:
time: 154 us
  blocking collectives  52.3 us (34%)
  starting transfers between devices  39.8 us (26%)
  waiting for transfers between devices  27.4 us (18%)
  Pallas kernels  26.8 us (17%)
  local copies, waits for them, and re-layouts  2.67 us (2%)
  other arithmetic  2.4 us (2%)
  between operations  2.13 us (1%)
    all_to_all x3, blocking collectives, over_dp(): lax.all_to_all(jnp.broadcast_to(both[None], (NXY, LROWS, BLOCK)), ('x', '...  32.9 us
    all_to_all x2, blocking collectives, over_noise(): return lax.all_to_all(pieces, 'z', 0, 0, tiled=True)  19.5 us
    ppermute x3, starting transfers between devices, on_device(): own = [mine] + [lax.ppermute(mine, 'z', shifted(2 * q)) for q in (1, 2, 3)]  10.5 us
    ppermute x1, waiting for transfers between devices, on_device(): paired = lax.ppermute(away, 'z', PAIRS)  9.39 us
    ppermute x3, starting transfers between devices, over_dp(): came = lax.ppermute(lse, 'c', CORES)  7.99 us
    ppermute x3, starting transfers between devices, on_device(): lax.ppermute(summed[q], 'z', shifted(2 * q))  7.74 us
    ppermute x3, waiting for transfers between devices, on_device(): lax.ppermute(summed[q], 'z', shifted(2 * q))  7.01 us
    pallas_call x1, Pallas kernels, on_device(): call(project_noise_body, [pltpu.HBM((NZ // 2, CB * CHUNK, BLOCK), F32) fo...  6.45 us
  transfers between devices with their start and end apart: 15, of which 10 were waited for; matrix products, arithmetic and copies ran while one was open for 1% of the time, Pallas kernels for 10%

profile of v4, /device:TPU:1, one launch (start us, length us, event | category | flops | bytes accessed | tf_op | source)
XLA Modules:
  0.0 153.5 jit_solution(15182026316104990396)
XLA Ops:
  0.6 3.9 %collective-permute-start = (f32[64,384]{1,0:T(8,128)}, f32[64,384]{1,0:T(8,128)S(1)}, u32[]{:S(2)}, u32[]{:S(2)}) collective-permute-start(f32[64,384]{1,0:T(8,128)} %bitcast.7), channel_id=1, source_target_pairs={{0,64},{32,96},{64,128},{96,160},{128,192},{160,224},{192,0},{224,... | collective-permute-start | bytes 294920 | tf_op jit(solution)/shard_map/ppermute | solution.py:380
  4.5 3.1 %collective-permute-start.2 = (f32[64,384]{1,0:T(8,128)}, f32[64,384]{1,0:T(8,128)S(1)}, u32[]{:S(2)}, u32[]{:S(2)}) collective-permute-start(f32[64,384]{1,0:T(8,128)} %bitcast.8), channel_id=1, source_target_pairs={{0,192},{32,224},{64,0},{96,32},{128,64},{160,96},{192,128},{224,1... | collective-permute-start | bytes 294920 | tf_op jit(solution)/shard_map/ppermute | solution.py:380
  7.6 2.7 %collective-permute-done.refs_1_ = f32[64,384]{1,0:T(8,128)S(1)} collective-permute-done((f32[64,384]{1,0:T(8,128)}, f32[64,384]{1,0:T(8,128)S(1)}, u32[]{:S(2)}, u32[]{:S(2)}) %collective-permute-start) | collective-permute-done | bytes 98336 | tf_op jit(solution)/shard_map/ppermute | solution.py:380
  10.3 3.6 %collective-permute-done.2.refs_3_ = f32[64,384]{1,0:T(8,128)S(1)} collective-permute-done((f32[64,384]{1,0:T(8,128)}, f32[64,384]{1,0:T(8,128)S(1)}, u32[]{:S(2)}, u32[]{:S(2)}) %collective-permute-start.2) | collective-permute-done | bytes 98336 | tf_op jit(solution)/shard_map/ppermute | solution.py:380
  13.9 0.0 copy-start.1
  13.9 1.0 pad_maximum_fusion
  14.9 0.1 collective-permute-start.3
  15.0 2.7 %collective-permute-start.4 = (f32[128,384]{1,0:T(8,128)S(1)}, f32[128,384]{1,0:T(8,128)S(1)}, u32[]{:S(2)}, u32[]{:S(2)}) collective-permute-start(f32[128,384]{1,0:T(8,128)S(1)} %get-tuple-element.62), channel_id=1, source_target_pairs={{0,224},{32,0},{64,32},{96,64},{128,96},{160,128},{192,160},{224,1... | collective-permute-start | bytes 589832 | tf_op jit(solution)/shard_map/ppermute | solution.py:382
  17.6 3.5 %collective-permute-start.1 = (f32[64,384]{1,0:T(8,128)}, f32[64,384]{1,0:T(8,128)S(1)}, u32[]{:S(2)}, u32[]{:S(2)}) collective-permute-start(f32[64,384]{1,0:T(8,128)} %bitcast.10), channel_id=1, source_target_pairs={{0,128},{32,160},{64,192},{96,224},{128,0},{160,32},{192,64},{224,... | collective-permute-start | bytes 294920 | tf_op jit(solution)/shard_map/ppermute | solution.py:380
  22.5 0.0 copy-start
  22.5 1.9 %copy-done = f32[1536,512]{1,0:T(8,128)S(1)} copy-done((f32[1536,512]{1,0:T(8,128)S(1)}, f32[1536,512]{1,0:T(8,128)}, u32[]{:S(2)}) %copy-start) | copy-done | bytes 3145752
  24.3 4.6 %shard_map.75 = (bf16[2,1536,256]{2,1,0:T(8,128)(2,1)S(1)}, bf16[2,1536,256]{2,1,0:T(8,128)(2,1)S(1)}, bf16[512,1536]{1,0:T(8,128)(2,1)}, bf16[512,1536]{1,0:T(8,128)(2,1)}, f32[1536,1]{1,0:T(8,128)S(1)}) custom-call(s32[1]{0:T(128)} %bitcast.2.place, s32[1]{0:T(128)} %bitcast.3.core, s32[1]{0:T(128)S(6)} %copy.8.nblk, s32[1]{0:T(128)S(6)} %copy.9.dblk, ...), custom_call_target="tpu_custom_call" | custom-call | flops 1000000 | bytes 4000000 | tf_op jit(solution)/shard_map/pallas_call | solution.py:383
  28.9 0.0 collective-permute-done.1.refs_2_
  28.9 0.0 copy-done.1
  28.9 1.5 shard_map.76.near
  30.4 0.0 collective-permute-done.3.left
  30.4 0.0 collective-permute-done.4.right
  30.4 1.9 %shard_map.77 = (f32[1536,384]{1,0:T(8,128)S(1)}, f32[16,128]{1,0:T(8,128)S(1)}, bf16[2,2,256,384]{3,2,1,0:T(8,128)(2,1)S(1)}) custom-call(s32[1]{0:T(128)} %bitcast.2.place, s32[1]{0:T(128)S(6)} %copy.9.dblk, bf16[2,1536,256]{2,1,0:T(8,128)(2,1)S(1)} %get-tuple-element.35.high, bf16[2,1536,256]{2,1,0:T(8,128)(2,1)S(1)} %get-tuple-element.36.low, ...), custom_call_target="tpu_custom_call" | custom-call | flops 1000000 | bytes 4000000 | tf_op jit(solution)/shard_map/pallas_call | solution.py:408
  32.3 1.7 %collective-permute-start.5 = (f32[16,128]{1,0:T(8,128)S(1)}, f32[16,128]{1,0:T(8,128)S(1)}, u32[]{:S(2)}, u32[]{:S(2)}) collective-permute-start(f32[16,128]{1,0:T(8,128)S(1)} %get-tuple-element.39), channel_id=1, source_target_pairs={{0,1},{1,0},{2,3},{3,2},{4,5},{5,4},{6,7},{7,6},{8,9},{9,8},{10,11... | collective-permute-start | bytes 24584 | tf_op jit(solution)/shard_map/ppermute | solution.py:362
  34.0 0.8 collective-permute-done.5
  34.9 0.1 add_select_fusion.2
  34.9 13.2 %all_to_all.35.got = f32[16,16,128]{2,1,0:T(8,128)S(1)} all-to-all(f32[16,16,128]{2,1,0:T(8,128)S(1)} %broadcast_in_dim.12), channel_id=1, replica_groups=mesh['z'=8,'x'=4,'y'=4,'c'=2] {'x','y'}, dimensions={0} | all-to-all | bytes 262144 | tf_op jit(solution)/shard_map/all_to_all | solution.py:367
  48.2 0.8 shard_map.78
  49.0 10.2 %all_to_all.36.got = f32[8,8,128]{2,1,0:T(8,128)S(1)} all-to-all(f32[8,8,128]{2,1,0:T(8,128)S(1)} %get-tuple-element.41), channel_id=1, replica_groups=mesh['z'=8,'x'=4,'y'=4,'c'=2] {'z'}, dimensions={0} | all-to-all | bytes 65536 | tf_op jit(solution)/shard_map/all_to_all | solution.py:373
  59.2 1.0 shard_map.79
  60.2 3.3 %collective-permute-start.6 = (f32[16,128]{1,0:T(8,128)S(1)}, f32[16,128]{1,0:T(8,128)S(1)}, u32[]{:S(2)}, u32[]{:S(2)}) collective-permute-start(f32[16,128]{1,0:T(8,128)S(1)} %shard_map.79), channel_id=1, source_target_pairs={{0,1},{1,0},{2,3},{3,2},{4,5},{5,4},{6,7},{7,6},{8,9},{9,8},{10,11... | collective-permute-start | bytes 24584 | tf_op jit(solution)/shard_map/ppermute | solution.py:362
  63.5 0.8 collective-permute-done.6
  64.3 0.1 add_select_fusion.1
  64.4 9.8 %all_to_all.37.got = f32[16,16,128]{2,1,0:T(8,128)S(1)} all-to-all(f32[16,16,128]{2,1,0:T(8,128)S(1)} %broadcast_in_dim.14), channel_id=1, replica_groups=mesh['z'=8,'x'=4,'y'=4,'c'=2] {'x','y'}, dimensions={0} | all-to-all | bytes 262144 | tf_op jit(solution)/shard_map/all_to_all | solution.py:367
  74.2 0.8 shard_map.80
  75.0 9.2 %all_to_all.38.got = f32[8,8,128]{2,1,0:T(8,128)S(1)} all-to-all(f32[8,8,128]{2,1,0:T(8,128)S(1)} %get-tuple-element.42), channel_id=1, replica_groups=mesh['z'=8,'x'=4,'y'=4,'c'=2] {'z'}, dimensions={0} | all-to-all | bytes 65536 | tf_op jit(solution)/shard_map/all_to_all | solution.py:373
  84.3 1.0 shard_map.81
  85.3 3.0 %collective-permute-start.7 = (f32[16,128]{1,0:T(8,128)S(1)}, f32[16,128]{1,0:T(8,128)S(1)}, u32[]{:S(2)}, u32[]{:S(2)}) collective-permute-start(f32[16,128]{1,0:T(8,128)S(1)} %shard_map.81), channel_id=1, source_target_pairs={{0,1},{1,0},{2,3},{3,2},{4,5},{5,4},{6,7},{7,6},{8,9},{9,8},{10,11... | collective-permute-start | bytes 24584 | tf_op jit(solution)/shard_map/ppermute | solution.py:362
  88.3 0.8 collective-permute-done.7
  89.1 0.1 add_select_fusion
  89.2 9.8 %all_to_all.39.got = f32[16,16,128]{2,1,0:T(8,128)S(1)} all-to-all(f32[16,16,128]{2,1,0:T(8,128)S(1)} %broadcast_in_dim.28), channel_id=1, replica_groups=mesh['z'=8,'x'=4,'y'=4,'c'=2] {'x','y'}, dimensions={0} | all-to-all | bytes 262144 | tf_op jit(solution)/shard_map/all_to_all | solution.py:367
  99.0 1.4 shard_map.82
  100.4 3.3 %all-to-all-start.5 = ((f32[8,8,128]{2,1,0:T(8,128)}), f32[8,8,128]{2,1,0:T(8,128)S(1)}, u32[]{:S(2)}, u32[]{:S(2)}) async-start(f32[8,8,128]{2,1,0:T(8,128)} %get-tuple-element.44.own), calls=%async_computation.5 | async-start | bytes 65536 | tf_op jit(solution)/shard_map/all_to_all | solution.py:373
  103.7 6.4 %shard_map.83 = (f32[4,192,128]{2,1,0:T(8,128)}, f32[4,192,128]{2,1,0:T(8,128)}) custom-call(s32[1]{0:T(128)} %bitcast.2.place, s32[1]{0:T(128)S(6)} %copy.8.nblk, f32[8,8,128]{2,1,0:T(8,128)} %get-tuple-element.44.own, f32[16,128]{1,0:T(8,128)S(1)} %get-tuple-element.43.dual, f32[1536,384]{1,0:T(8,128)S(1)} %get-tuple-element.40.cost, ...), custom_call_target="tpu_custom_call" | custom-call | flops 1000000 | bytes 4000000 | tf_op jit(solution)/shard_map/pallas_call | solution.py:426
  110.2 0.3 all-to-all-done.5.got
  110.5 1.9 %shard_map.84 = (f32[16,216,128]{2,1,0:T(8,128)S(1)}, bf16[1536,384]{1,0:T(8,128)(2,1)S(1)}, bf16[1536,384]{1,0:T(8,128)(2,1)S(1)}, f32[1,384]{1,0:T(1,128)S(1)}, f32[24,128]{1,0:T(8,128)S(1)}) custom-call(s32[1]{0:T(128)} %bitcast.3.core, s32[1]{0:T(128)S(6)} %copy.9.dblk, f32[8,8,128]{2,1,0:T(8,128)S(1)} %all-to-all-done.5.got, ...), custom_call_target="tpu_custom_call" | custom-call | flops 1000000 | bytes 4000000 | tf_op jit(solution)/shard_map/pallas_call | solution.py:461
  112.5 3.0 %collective-permute-start.8 = (f32[16,216,128]{2,1,0:T(8,128)S(1)}, f32[16,216,128]{2,1,0:T(8,128)S(1)}, u32[]{:S(2)}, u32[]{:S(2)}) collective-permute-start(f32[16,216,128]{2,1,0:T(8,128)S(1)} %get-tuple-element.55), channel_id=1, source_target_pairs={{0,1},{1,0},{2,3},{3,2},{4,5},{5,4},{6,7},{7,6},{8,9},{9,8},{10,11... | collective-permute-start | bytes 5308424 | tf_op jit(solution)/shard_map/ppermute | solution.py:472
  115.5 1.4 shard_map.85.own
  116.9 1.9 %collective-permute-done.8.came = f32[16,216,128]{2,1,0:T(8,128)S(1)} collective-permute-done((f32[16,216,128]{2,1,0:T(8,128)S(1)}, f32[16,216,128]{2,1,0:T(8,128)S(1)}, u32[]{:S(2)}, u32[]{:S(2)}) %collective-permute-start.8) | collective-permute-done | bytes 1769504 | tf_op jit(solution)/shard_map/ppermute | solution.py:472
  118.8 1.4 shard_map.86
  120.2 0.0 copy-start.3
  120.3 3.8 %all-to-all-start.6 = ((f32[16,208,128]{2,1,0:T(8,128)}), f32[16,208,128]{2,1,0:T(8,128)S(1)}, u32[]{:S(2)}, u32[]{:S(2)}) async-start(f32[16,208,128]{2,1,0:T(8,128)} %shard_map.86), calls=%async_computation.6 | async-start | bytes 3407872 | tf_op jit(solution)/shard_map/all_to_all | solution.py:477
  124.1 0.0 copy-done.3
  124.1 0.6 collective-permute-start.9
  124.7 0.6 bitcast_select_fusion
  125.3 9.4 %collective-permute-done.9.came = f32[4,192,128]{2,1,0:T(8,128)S(1)} collective-permute-done((f32[4,192,128]{2,1,0:T(8,128)S(1)}, f32[4,192,128]{2,1,0:T(8,128)S(1)}, u32[]{:S(2)}, u32[]{:S(2)}) %collective-permute-start.9) | collective-permute-done | bytes 393248 | tf_op jit(solution)/shard_map/ppermute | solution.py:449
  134.7 0.0 copy-start.2
  134.7 0.7 copy-done.2
  135.5 1.2 shard_map.88
  136.7 1.1 collective-permute-start.10
  137.8 3.3 %collective-permute-start.11 = (f32[192,128]{1,0:T(8,128)S(1)}, f32[192,128]{1,0:T(8,128)S(1)}, u32[]{:S(2)}, u32[]{:S(2)}) collective-permute-start(f32[192,128]{1,0:T(8,128)S(1)} %get-tuple-element.60), channel_id=1, source_target_pairs={{0,128},{32,160},{64,192},{96,224},{128,0},{160,32},{192,64},{224,... | collective-permute-start | bytes 294920 | tf_op jit(solution)/shard_map/ppermute | solution.py:459
  141.1 3.3 %collective-permute-start.12 = (f32[192,128]{1,0:T(8,128)S(1)}, f32[192,128]{1,0:T(8,128)S(1)}, u32[]{:S(2)}, u32[]{:S(2)}) collective-permute-start(f32[192,128]{1,0:T(8,128)S(1)} %get-tuple-element.61), channel_id=1, source_target_pairs={{0,192},{32,224},{64,0},{96,32},{128,64},{160,96},{192,128},{224,1... | collective-permute-start | bytes 294920 | tf_op jit(solution)/shard_map/ppermute | solution.py:459
  144.4 0.6 fusion.3
  145.0 0.0 collective-permute-done.10.refs_1_
  145.0 3.3 %collective-permute-done.11.refs_2_ = f32[192,128]{1,0:T(8,128)S(1)} collective-permute-done((f32[192,128]{1,0:T(8,128)S(1)}, f32[192,128]{1,0:T(8,128)S(1)}, u32[]{:S(2)}, u32[]{:S(2)}) %collective-permute-start.11) | collective-permute-done | bytes 98336 | tf_op jit(solution)/shard_map/ppermute | solution.py:459
  148.3 3.7 %collective-permute-done.12.refs_3_ = f32[192,128]{1,0:T(8,128)S(1)} collective-permute-done((f32[192,128]{1,0:T(8,128)S(1)}, f32[192,128]{1,0:T(8,128)S(1)}, u32[]{:S(2)}, u32[]{:S(2)}) %collective-permute-start.12) | collective-permute-done | bytes 98336 | tf_op jit(solution)/shard_map/ppermute | solution.py:459
  152.0 0.7 shard_map.89
  152.7 0.0 all-to-all-done.6.came
  152.7 0.9 shard_map.87
  (5 shorter events, 0.1 us)
Async XLA Ops:
  0.6 9.7 %collective-permute-start = (f32[64,384]{1,0:T(8,128)}, f32[64,384]{1,0:T(8,128)S(1)}, u32[]{:S(2)}, u32[]{:S(2)}) collective-permute-start(f32[64,384]{1,0:T(8,128)} %bitcast.7), channel_id=1, source_target_pairs={{0,64},{32,96},{64,128},{96,160},{128,192},{160,224},{192,0},{224,... | collective-permute-start | bytes 294920 | tf_op jit(solution)/shard_map/ppermute | solution.py:380
  4.5 9.4 %collective-permute-start.2 = (f32[64,384]{1,0:T(8,128)}, f32[64,384]{1,0:T(8,128)S(1)}, u32[]{:S(2)}, u32[]{:S(2)}) collective-permute-start(f32[64,384]{1,0:T(8,128)} %bitcast.8), channel_id=1, source_target_pairs={{0,192},{32,224},{64,0},{96,32},{128,64},{160,96},{192,128},{224,1... | collective-permute-start | bytes 294920 | tf_op jit(solution)/shard_map/ppermute | solution.py:380
  13.9 15.0 %copy-start.1 = (f32[384,64]{0,1:T(8,128)S(1)}, f32[384,64]{0,1:T(8,128)}, u32[]{:S(2)}) copy-start(f32[384,64]{0,1:T(8,128)} %param.5) | copy-start | bytes 294916
  14.9 15.5 %collective-permute-start.3 = (f32[128,384]{1,0:T(8,128)S(1)}, f32[128,384]{1,0:T(8,128)S(1)}, u32[]{:S(2)}, u32[]{:S(2)}) collective-permute-start(f32[128,384]{1,0:T(8,128)S(1)} %get-tuple-element.63), channel_id=1, source_target_pairs={{0,32},{32,64},{64,96},{96,128},{128,160},{160,192},{192,224},{224... | collective-permute-start | bytes 589832 | tf_op jit(solution)/shard_map/ppermute | solution.py:381
  15.0 15.4 %collective-permute-start.4 = (f32[128,384]{1,0:T(8,128)S(1)}, f32[128,384]{1,0:T(8,128)S(1)}, u32[]{:S(2)}, u32[]{:S(2)}) collective-permute-start(f32[128,384]{1,0:T(8,128)S(1)} %get-tuple-element.62), channel_id=1, source_target_pairs={{0,224},{32,0},{64,32},{96,64},{128,96},{160,128},{192,160},{224,1... | collective-permute-start | bytes 589832 | tf_op jit(solution)/shard_map/ppermute | solution.py:382
  17.6 11.3 %collective-permute-start.1 = (f32[64,384]{1,0:T(8,128)}, f32[64,384]{1,0:T(8,128)S(1)}, u32[]{:S(2)}, u32[]{:S(2)}) collective-permute-start(f32[64,384]{1,0:T(8,128)} %bitcast.10), channel_id=1, source_target_pairs={{0,128},{32,160},{64,192},{96,224},{128,0},{160,32},{192,64},{224,... | collective-permute-start | bytes 294920 | tf_op jit(solution)/shard_map/ppermute | solution.py:380
  22.5 1.9 %copy-start = (f32[1536,512]{1,0:T(8,128)S(1)}, f32[1536,512]{1,0:T(8,128)}, u32[]{:S(2)}) copy-start(f32[1536,512]{1,0:T(8,128)} %points.1) | copy-start | bytes 9437188
  32.3 2.5 %collective-permute-start.5 = (f32[16,128]{1,0:T(8,128)S(1)}, f32[16,128]{1,0:T(8,128)S(1)}, u32[]{:S(2)}, u32[]{:S(2)}) collective-permute-start(f32[16,128]{1,0:T(8,128)S(1)} %get-tuple-element.39), channel_id=1, source_target_pairs={{0,1},{1,0},{2,3},{3,2},{4,5},{5,4},{6,7},{7,6},{8,9},{9,8},{10,11... | collective-permute-start | bytes 24584 | tf_op jit(solution)/shard_map/ppermute | solution.py:362
  60.2 4.1 %collective-permute-start.6 = (f32[16,128]{1,0:T(8,128)S(1)}, f32[16,128]{1,0:T(8,128)S(1)}, u32[]{:S(2)}, u32[]{:S(2)}) collective-permute-start(f32[16,128]{1,0:T(8,128)S(1)} %shard_map.79), channel_id=1, source_target_pairs={{0,1},{1,0},{2,3},{3,2},{4,5},{5,4},{6,7},{7,6},{8,9},{9,8},{10,11... | collective-permute-start | bytes 24584 | tf_op jit(solution)/shard_map/ppermute | solution.py:362
  85.3 3.8 %collective-permute-start.7 = (f32[16,128]{1,0:T(8,128)S(1)}, f32[16,128]{1,0:T(8,128)S(1)}, u32[]{:S(2)}, u32[]{:S(2)}) collective-permute-start(f32[16,128]{1,0:T(8,128)S(1)} %shard_map.81), channel_id=1, source_target_pairs={{0,1},{1,0},{2,3},{3,2},{4,5},{5,4},{6,7},{7,6},{8,9},{9,8},{10,11... | collective-permute-start | bytes 24584 | tf_op jit(solution)/shard_map/ppermute | solution.py:362
  100.4 10.1 %all-to-all-start.5 = ((f32[8,8,128]{2,1,0:T(8,128)}), f32[8,8,128]{2,1,0:T(8,128)S(1)}, u32[]{:S(2)}, u32[]{:S(2)}) async-start(f32[8,8,128]{2,1,0:T(8,128)} %get-tuple-element.44.own), calls=%async_computation.5 | async-start | bytes 65536 | tf_op jit(solution)/shard_map/all_to_all | solution.py:373
  112.5 6.3 %collective-permute-start.8 = (f32[16,216,128]{2,1,0:T(8,128)S(1)}, f32[16,216,128]{2,1,0:T(8,128)S(1)}, u32[]{:S(2)}, u32[]{:S(2)}) collective-permute-start(f32[16,216,128]{2,1,0:T(8,128)S(1)} %get-tuple-element.55), channel_id=1, source_target_pairs={{0,1},{1,0},{2,3},{3,2},{4,5},{5,4},{6,7},{7,6},{8,9},{9,8},{10,11... | collective-permute-start | bytes 5308424 | tf_op jit(solution)/shard_map/ppermute | solution.py:472
  120.2 3.9 %copy-start.3 = (f32[4,192,128]{2,1,0:T(8,128)S(1)}, f32[4,192,128]{2,1,0:T(8,128)}, u32[]{:S(2)}) copy-start(f32[4,192,128]{2,1,0:T(8,128)} %get-tuple-element.57) | copy-start | bytes 1179652
  120.3 32.4 %all-to-all-start.6 = ((f32[16,208,128]{2,1,0:T(8,128)}), f32[16,208,128]{2,1,0:T(8,128)S(1)}, u32[]{:S(2)}, u32[]{:S(2)}) async-start(f32[16,208,128]{2,1,0:T(8,128)} %shard_map.86), calls=%async_computation.6 | async-start | bytes 3407872 | tf_op jit(solution)/shard_map/all_to_all | solution.py:477
  124.1 10.6 %collective-permute-start.9 = (f32[4,192,128]{2,1,0:T(8,128)S(1)}, f32[4,192,128]{2,1,0:T(8,128)S(1)}, u32[]{:S(2)}, u32[]{:S(2)}) collective-permute-start(f32[4,192,128]{2,1,0:T(8,128)S(1)} %copy-done.3), channel_id=1, source_target_pairs={{0,32},{32,0},{64,96},{96,64},{128,160},{160,128},{192,224},{224,1... | collective-permute-start | bytes 1179656 | tf_op jit(solution)/shard_map/ppermute | solution.py:449
  134.7 0.7 copy-start.2
  136.7 8.3 %collective-permute-start.10 = (f32[192,128]{1,0:T(8,128)S(1)}, f32[192,128]{1,0:T(8,128)S(1)}, u32[]{:S(2)}, u32[]{:S(2)}) collective-permute-start(f32[192,128]{1,0:T(8,128)S(1)} %get-tuple-element.59), channel_id=1, source_target_pairs={{0,64},{32,96},{64,128},{96,160},{128,192},{160,224},{192,0},{224,... | collective-permute-start | bytes 294920 | tf_op jit(solution)/shard_map/ppermute | solution.py:459
  137.8 10.5 %collective-permute-start.11 = (f32[192,128]{1,0:T(8,128)S(1)}, f32[192,128]{1,0:T(8,128)S(1)}, u32[]{:S(2)}, u32[]{:S(2)}) collective-permute-start(f32[192,128]{1,0:T(8,128)S(1)} %get-tuple-element.60), channel_id=1, source_target_pairs={{0,128},{32,160},{64,192},{96,224},{128,0},{160,32},{192,64},{224,... | collective-permute-start | bytes 294920 | tf_op jit(solution)/shard_map/ppermute | solution.py:459
  141.1 10.9 %collective-permute-start.12 = (f32[192,128]{1,0:T(8,128)S(1)}, f32[192,128]{1,0:T(8,128)S(1)}, u32[]{:S(2)}, u32[]{:S(2)}) collective-permute-start(f32[192,128]{1,0:T(8,128)S(1)} %get-tuple-element.61), channel_id=1, source_target_pairs={{0,192},{32,224},{64,0},{96,32},{128,64},{160,96},{192,128},{224,1... | collective-permute-start | bytes 294920 | tf_op jit(solution)/shard_map/ppermute | solution.py:459
